TPU v7x, 256 devices: a whole 4x4x8 slice. The times are simulated.
256 devices in a mesh: gx: 4 (over z_hi), gy: 4 (over z_lo, core), gz: 16 (over y, x).
Axes of the slice: x: 4, y: 4, z: 8 (z_hi: 4, z_lo: 2; z = z_hi * 2 + z_lo), core: 2. Of those that a mesh axis runs over, the one named last changes fastest.
Arguments:
- populations: float32 [19, 128, 128, 512], P(None, 'gz', 'gy', 'gx'), as said below
- rbf_weights: bfloat16 [16384, 128, 128], P(('gx', 'gy', 'gz')), may hold values from -0.5 to 0.5
- owner_map: int32 [16384, 1], P(('gx', 'gy', 'gz')), may hold values from 0 to 63; in each aligned block of 64 rows (0 to 63, 64 to 127, ...) at most 2 rows name the same one
- shell_slot: int32 [16384, 1], P(('gx', 'gy', 'gz')), may hold values from 0 to 7
- compliance: float32 [2048, 128, 128], P(('gx', 'gy', 'gz')), may hold values from -0.5 to 0.5
- neighbour_compliance: float32 [32768, 128], P(('gx', 'gy', 'gz')), may hold values from -0.5 to 0.5
- interface_row: int32 [16384], P(('gx', 'gy', 'gz')), may hold values from 0 to 255, as said below
Outputs:
- new_populations: float32 [19, 128, 128, 512], P(None, 'gz', 'gy', 'gx')
- displacement: float32 [2048, 3, 128], P(('gx', 'gy', 'gz'))
- wall_motion: float32 [16384, 3, 128], P(('gx', 'gy', 'gz'))
Inputs may be any that keep to these rules, and one draw needn't show every extreme that they name: `populations`: each population lies between 0.5 and 1.5 times its lattice weight. `owner_map`: among the 64 rows of one device no owner appears more than 2 times, and some owner appears exactly 2 times. `interface_row`: the 64 rows of one device are distinct.
All inputs are finite; a program needn't handle non-finite values.
Results may differ from a plain program's by a relative error of at most 0.004.
Values sent between devices are 32-bit elements; how exact they have to be, the bound alone decides.
No kernel may reach another device: no remote copies, remote signals or barrier semaphores. Data moves between devices by JAX's collectives and lax.ppermute only.
A program may use at most 64 MiB of HBM per device.

v0:
```python
import math

import jax
import jax.numpy as jnp
from jax import lax
from jax.sharding import PartitionSpec as P

lattice_velocity = (
    (0, 0, 0),
    (1, 0, 0),
    (-1, 0, 0),
    (0, 1, 0),
    (0, -1, 0),
    (0, 0, 1),
    (0, 0, -1),
    (1, 1, 0),
    (-1, -1, 0),
    (1, -1, 0),
    (-1, 1, 0),
    (1, 0, 1),
    (-1, 0, -1),
    (1, 0, -1),
    (-1, 0, 1),
    (0, 1, 1),
    (0, -1, -1),
    (0, 1, -1),
    (0, -1, 1),
)
lattice_weight = (1.0 / 3.0,) + (1.0 / 18.0,) * 6 + (1.0 / 36.0,) * 12
load_scale = 30.0
relaxation = 1.6


def from_behind(value, axis, steps):
    count = lax.axis_size(axis)
    pairs = [(source, (source + steps) % count) for source in range(count)]
    return lax.ppermute(value, axis, pairs)


def in_one_piece(arrays, axis, split_dim, concat_dim, along):
    widths = [math.prod(a.shape[along:]) for a in arrays]
    both = jnp.concatenate(
        [a.reshape(*a.shape[:along], w) for a, w in zip(arrays, widths)], axis=along
    )
    filled = lax.all_to_all(both, axis, split_axis=split_dim, concat_axis=concat_dim, tiled=True)
    blocks = jnp.split(filled, [sum(widths[:k]) for k in range(1, len(widths))], axis=along)
    return tuple(
        (b.reshape(*filled.shape[:along], *a.shape[along:]) for a, b in zip(arrays, blocks))
    )


def from_behind_2(array, axis, by):
    peers = lax.axis_size(axis)
    pairs = [(i, i + by) for i in range(peers) if 0 <= i + by < peers]
    return lax.ppermute(array, axis, pairs)


def moment_matrix():
    return jnp.array(
        [
            [1.0] * 19,
            [float(item[0]) for item in lattice_velocity],
            [float(item[1]) for item in lattice_velocity],
            [float(item[2]) for item in lattice_velocity],
        ],
        dtype=jnp.float32,
    )


def collide(flattened):
    moments = jnp.dot(moment_matrix(), flattened, precision=lax.Precision.HIGHEST)
    density = moments[0]
    velocity = moments[1:4] / density
    speed_square = velocity[0] * velocity[0] + velocity[1] * velocity[1] + velocity[2] * velocity[2]
    relaxed = []
    for direction in range(19):
        along_x, along_y, along_z = lattice_velocity[direction]
        projected = along_x * velocity[0] + along_y * velocity[1] + along_z * velocity[2]
        equilibrium = (
            lattice_weight[direction]
            * density
            * (1.0 + 3.0 * projected + 4.5 * projected * projected - 1.5 * speed_square)
        )
        relaxed.append(flattened[direction] - relaxation * (flattened[direction] - equilibrium))
    return (relaxed, moments)


def signed_set(component, sign):
    return [direction for direction in range(19) if lattice_velocity[direction][component] == sign]


def edge_layers(current, component, sign, field_dim):
    length = current[0].shape[field_dim]
    start = length - 1 if sign > 0 else 0
    return jnp.stack(
        [
            lax.slice_in_dim(current[direction], start, start + 1, axis=field_dim)
            for direction in signed_set(component, sign)
        ]
    )


def roll_in_layers(current, component, field_dim, from_below, from_above):
    length = current[0].shape[field_dim]
    position = lax.broadcasted_iota(jnp.int32, current[0].shape, field_dim)
    updated = list(current)
    for index, direction in enumerate(signed_set(component, 1)):
        moved = jnp.roll(current[direction], 1, axis=field_dim)
        updated[direction] = jnp.where(position == 0, from_below[index], moved)
    for index, direction in enumerate(signed_set(component, -1)):
        moved = jnp.roll(current[direction], -1, axis=field_dim)
        updated[direction] = jnp.where(position == length - 1, from_above[index], moved)
    return updated


def body(
    populations, rbf_weights, owner_map, shell_slot, compliance, neighbour_compliance, interface_row
):
    local_shape = populations.shape[1:]
    depth, height, width = local_shape
    relaxed, moments = collide(populations.reshape(19, -1))
    relaxed = [item.reshape(local_shape) for item in relaxed]
    current = relaxed
    below_x = from_behind(edge_layers(current, 0, 1, 2), "gx", 1)
    above_x = from_behind(edge_layers(current, 0, -1, 2), "gx", -1)
    current = roll_in_layers(current, 0, 2, below_x, above_x)
    below_y = from_behind(edge_layers(current, 1, 1, 1), "gy", 1)
    above_y = from_behind(edge_layers(current, 1, -1, 1), "gy", -1)
    current = roll_in_layers(current, 1, 1, below_y, above_y)
    below_z = from_behind(edge_layers(current, 2, 1, 0), "gz", 1)
    above_z = from_behind(edge_layers(current, 2, -1, 0), "gz", -1)
    current = roll_in_layers(current, 2, 0, below_z, above_z)
    new_populations = jnp.stack(current)
    block_count = rbf_weights.shape[0]
    node_count = rbf_weights.shape[2]
    shell_count = compliance.shape[0]
    pencils = lax.axis_size("gy")
    blocks_z = lax.axis_size("gz")
    owner_count = pencils * blocks_z
    capacity = max(2, 2 * block_count // owner_count)
    slots = owner_count * capacity
    momentum = moments[1:4].reshape(3, depth * height, width)
    interface_momentum = jnp.take(momentum, interface_row, axis=1)
    traction = (load_scale * interface_momentum).astype(jnp.bfloat16)
    forces = jnp.einsum("kbc,bcs->bks", traction, rbf_weights, preferred_element_type=jnp.float32)
    forces = forces.reshape(block_count, 3 * node_count)
    owner_of = owner_map[:, 0]
    owner_onehot = (owner_of[:, None] == jnp.arange(owner_count, dtype=jnp.int32)[None, :]).astype(
        jnp.float32
    )
    running = jnp.cumsum(owner_onehot, axis=0) - owner_onehot
    slot_rank = jnp.sum(running * owner_onehot, axis=1).astype(jnp.int32)
    slot_index = owner_of * capacity + slot_rank
    placement = (jnp.arange(slots, dtype=jnp.int32)[:, None] == slot_index[None, :]).astype(
        jnp.float32
    )
    outgoing = jnp.dot(placement, forces, precision=lax.Precision.HIGHEST)
    outgoing_tags = (
        jnp.dot(
            placement, (shell_slot[:, 0] + 1).astype(jnp.float32), precision=lax.Precision.HIGHEST
        )
        - 1.0
    )
    incoming, slot_tags = in_one_piece(
        (
            outgoing.reshape(owner_count, capacity, 3 * node_count),
            outgoing_tags.reshape(owner_count, capacity),
        ),
        ("gy", "gz"),
        0,
        0,
        2,
    )
    incoming = incoming.reshape(slots, 3 * node_count)
    slot_tags = slot_tags.reshape(slots)
    selector = (slot_tags[None, :] == jnp.arange(shell_count, dtype=jnp.float32)[:, None]).astype(
        jnp.float32
    )
    loads = jnp.dot(selector, incoming, precision=lax.Precision.HIGHEST).reshape(
        shell_count, 3, node_count
    )
    previous = from_behind_2(loads[shell_count - 1], ("gy", "gz"), 1)
    displacement = jnp.einsum("skn,snm->skm", loads, compliance, precision=lax.Precision.HIGHEST)
    shared_term = jnp.dot(previous, neighbour_compliance, precision=lax.Precision.HIGHEST)
    displacement = displacement.at[0].add(shared_term)
    returned = jnp.dot(
        selector.T,
        displacement.reshape(shell_count, 3 * node_count),
        precision=lax.Precision.HIGHEST,
    )
    arrived = lax.all_to_all(
        returned.reshape(owner_count, capacity, 3 * node_count),
        ("gy", "gz"),
        split_axis=0,
        concat_axis=0,
        tiled=True,
    )
    own_motion = jnp.dot(
        placement.T, arrived.reshape(slots, 3 * node_count), precision=lax.Precision.HIGHEST
    )
    own_motion = own_motion.reshape(block_count, 3, node_count).astype(jnp.bfloat16)
    wall_motion = jnp.einsum(
        "bks,bcs->bkc", own_motion, rbf_weights, preferred_element_type=jnp.float32
    )
    return (new_populations, displacement, wall_motion)


def solution(mesh):
    return jax.shard_map(
        body,
        mesh=mesh,
        in_specs=(
            P(None, "gz", "gy", "gx"),
            P(("gx", "gy", "gz"), None, None),
            P(("gx", "gy", "gz"), None),
            P(("gx", "gy", "gz"), None),
            P(("gx", "gy", "gz"), None, None),
            P(("gx", "gy", "gz"), None),
            P(("gx", "gy", "gz")),
        ),
        out_specs=(
            P(None, "gz", "gy", "gx"),
            P(("gx", "gy", "gz"), None, None),
            P(("gx", "gy", "gz"), None, None),
        ),
        check_vma=False,
    )
```

profile of v0, /device:TPU:1, one launch (start us, length us, event | category | flops | bytes accessed | tf_op | source)
XLA Modules:
  0.0 100.2 jit_solution(12172454663299424408)
XLA Ops:
  0.6 0.8 compare_and_fusion
  3.0 0.8 select_reduce_fusion
  4.5 0.8 fusion.2
  5.5 1.1 %copy.1883 = f32[64,2,1]{2,0,1:T(8,128)} copy(f32[64,2,1]{1,0,2:T(8,128)S(1)} %reshape_reshape.3) | data formatting | bytes 1024 | tf_op jit(solution)/shard_map/reshape;reshape | solution.py:43
  6.6 2.0 %pad.65 = f32[24,256,128]{2,1,0:T(8,128)S(1)} pad(f32[19,256,128]{2,1,0:T(8,128)} %bitcast.297, f32[]{:T(128)} %constant.66.clone.1), padding=0_5x0_0x0_0 | pad | bytes 5636100
  8.6 1.8 %copy.1892 = f32[3,8,256,128]{3,1,2,0:T(8,128)S(1)} copy(f32[3,8,256,128]{3,2,1,0:T(8,128)S(1)} %bitcast.296) | data formatting | bytes 6291456
  10.5 1.8 %fusion.184 = f32[4,32768]{1,0:T(4,128)S(1)} fusion(f32[4,19]{1,0:T(4,128)S(1)} %copy-done.6, f32[19,32768]{1,0:T(8,128)S(1)} %bitcast.295), kind=kOutput, calls=%fused_computation.390 | convolution fusion | flops 29884416 | bytes 3014960 | tf_op jit(solution)/shard_map/dot_general | solution.py:71
  12.9 1.3 %gather_fusion = f32[64,3,128]{2,1,0:T(4,128)} fusion(f32[3,256,128]{2,0,1:T(4,128)S(1)} %get-tuple-element.77, s32[1024]{0:T(1024)S(1)} %pad_clamp_fusion), kind=kCustom, calls=%fused_computation | custom fusion | bytes 196864 | tf_op jit(solution)/shard_map/jit(_take)/gather | solution.py:143
  14.2 1.6 %fusion.137 = f32[64,3,128]{2,1,0:T(4,128)S(1)} fusion(bf16[64,128,128]{2,1,0:T(8,128)(2,1)S(1)} %copy-done, f32[64,3,128]{2,1,0:T(4,128)} %gather_fusion, pred[64]{0:T(512)(128)(4,1)S(1)} %compare_and_fusion), kind=kOutput, calls=%fused_computation.264 | convolution fusion | flops 6365184 | bytes 2293824 | tf_op jit(solution)/shard_map/kbc,bcs->bks/dot_general | solution.py:145
  16.2 0.9 copy.1884
  17.1 10.3 %all-to-all-start = ((f32[64,2,385]{2,1,0:T(2,128)}), f32[64,2,385]{2,1,0:T(2,128)S(1)}, u32[]{:S(2)}, u32[]{:S(2)}) async-start(f32[64,2,385]{2,1,0:T(2,128)} %copy.1884), calls=%async_computation | async-start | bytes 524288 | tf_op jit(solution)/shard_map/all_to_all | solution.py:45
  28.0 1.2 %fusion.117 = (f32[8,32,128]{2,1,0:T(8,128)S(1)}, f32[8,32,128]{2,1,0:T(8,128)S(1)}) fusion(f32[8,32,128]{2,1,0:T(8,128)S(1)} %bitcast.308, f32[19,8,32,128]{3,2,1,0:T(8,128)} %param.10, f32[8,32,128]{2,1,0:T(8,128)S(1)} %bitcast.298, f32[8,32,128]{2,1,0:T(8,128)S(1)} %bitcast.305, f32[8,32,128]{2,1,0:T(8,128)S(1)} %bitcast.302), kind=kLoop, calls=%fused_computation.145 | loop fusion | flops 688128 | bytes 917504 | tf_op jit(solution)/shard_map/sub | solution.py:84
  29.2 1.5 %fusion.111 = (f32[8,32,128]{2,1,0:T(8,128)S(1)}, f32[8,32,128]{2,1,0:T(8,128)S(1)}, f32[8,32,128]{2,1,0:T(8,128)S(1)}, f32[8,32,128]{2,1,0:T(8,128)S(1)}, f32[8,32,128]{2,1,0:T(8,128)S(1)}) fusion(f32[8,32,128]{2,1,0:T(8,128)S(1)} %bitcast.309, f32[8,32,128]{2,1,0:T(8,128)S(1)} %get-tuple-element.52, f32[8,32,128]{2,1,0:T(8,128)S(1)} %bitcast.299, ...), kind=kLoop, calls=%fused_computation.139 | loop fusion | flops 2129920 | bytes 1966080 | tf_op jit(solution)/shard_map/sub | solution.py:84
  32.4 5.2 %collective-permute-start.1 = (f32[5,8,32,1]{2,1,3,0:T(8,128)S(1)}, f32[5,8,32,1]{2,1,3,0:T(8,128)S(1)}, u32[]{:S(2)}, u32[]{:S(2)}) collective-permute-start(f32[5,8,32,1]{2,1,3,0:T(8,128)S(1)} %constant_dynamic-update-slice_fusion.5), channel_id=1, source_target_pairs={{0,192},{64,0},{128,64},{192,128},{1,193},{65,1},{129,65},{193,129... | collective-permute-start | bytes 15368 | tf_op jit(solution)/shard_map/ppermute | solution.py:37
  38.5 0.7 slice_bitcast_fusion.11
  40.2 2.8 %collective-permute-done = f32[5,8,32,1]{2,1,3,0:T(8,128)S(1)} collective-permute-done((f32[5,8,32,1]{2,1,3,0:T(8,128)S(1)}, f32[5,8,32,1]{2,1,3,0:T(8,128)S(1)}, u32[]{:S(2)}, u32[]{:S(2)}) %collective-permute-start) | collective-permute-done | bytes 5152 | tf_op jit(solution)/shard_map/ppermute | solution.py:37
  43.6 3.1 %collective-permute-start.2 = (f32[5,8,1,128]{3,1,2,0:T(8,128)S(1)}, f32[5,8,1,128]{3,1,2,0:T(8,128)S(1)}, u32[]{:S(2)}, u32[]{:S(2)}) collective-permute-start(f32[5,8,1,128]{3,1,2,0:T(8,128)S(1)} %constant_dynamic-update-slice_fusion.10), channel_id=1, source_target_pairs={{0,16},{16,32},{32,48},{48,0},{1,17},{17,33},{33,49},{49,1},{2,18}... | collective-permute-start | bytes 61448 | tf_op jit(solution)/shard_map/ppermute | solution.py:37
  46.9 0.8 fusion.118
  47.7 0.8 fusion.119
  48.5 1.6 %collective-permute-done.3 = f32[5,8,1,128]{3,1,2,0:T(8,128)S(1)} collective-permute-done((f32[5,8,1,128]{3,1,2,0:T(8,128)S(1)}, f32[5,8,1,128]{3,1,2,0:T(8,128)S(1)}, u32[]{:S(2)}, u32[]{:S(2)}) %collective-permute-start.3) | collective-permute-done | bytes 20512 | tf_op jit(solution)/shard_map/ppermute | solution.py:37
  51.6 4.7 %collective-permute-start.5 = (f32[5,1,32,128]{3,2,1,0:T(8,128)S(1)}, f32[5,1,32,128]{3,2,1,0:T(8,128)S(1)}, u32[]{:S(2)}, u32[]{:S(2)}) collective-permute-start(f32[5,1,32,128]{3,2,1,0:T(8,128)S(1)} %constant_dynamic-update-slice_fusion.25), channel_id=1, source_target_pairs={{0,15},{1,0},{2,1},{3,2},{4,3},{5,4},{6,5},{7,6},{8,7},{9,8},{10,9... | collective-permute-start | bytes 245768 | tf_op jit(solution)/shard_map/ppermute | solution.py:37
  57.7 5.6 %collective-permute-done.4 = f32[5,1,32,128]{3,2,1,0:T(8,128)S(1)} collective-permute-done((f32[5,1,32,128]{3,2,1,0:T(8,128)S(1)}, f32[5,1,32,128]{3,2,1,0:T(8,128)S(1)}, u32[]{:S(2)}, u32[]{:S(2)}) %collective-permute-start.4) | collective-permute-done | bytes 81952 | tf_op jit(solution)/shard_map/ppermute | solution.py:37
  73.5 1.9 %collective-permute-start.6 = (f32[3,128]{1,0:T(4,128)S(1)}, f32[3,128]{1,0:T(4,128)S(1)}, u32[]{:S(2)}, u32[]{:S(2)}) collective-permute-start(f32[3,128]{1,0:T(4,128)S(1)} %bitcast.340), channel_id=1, source_target_pairs={{0,1},{1,2},{2,3},{3,4},{4,5},{5,6},{6,7},{7,8},{8,9},{9,10},{10,1... | collective-permute-start | bytes 4616 | tf_op jit(solution)/shard_map/ppermute | solution.py:55
  76.0 5.7 %collective-permute-done.6 = f32[3,128]{1,0:T(4,128)S(1)} collective-permute-done((f32[3,128]{1,0:T(4,128)S(1)}, f32[3,128]{1,0:T(4,128)S(1)}, u32[]{:S(2)}, u32[]{:S(2)}) %collective-permute-start.6) | collective-permute-done | bytes 1568 | tf_op jit(solution)/shard_map/ppermute | solution.py:55
  81.7 1.0 fusion.1
  83.1 0.8 copy.1887
  83.9 4.2 %all-to-all-start.1 = ((f32[64,2,384]{2,1,0:T(2,128)}), f32[64,2,384]{2,1,0:T(2,128)S(1)}, u32[]{:S(2)}, u32[]{:S(2)}) async-start(f32[64,2,384]{2,1,0:T(2,128)} %copy.1887), calls=%async_computation.1 | async-start | bytes 393216 | tf_op jit(solution)/shard_map/all_to_all | solution.py:191
  88.1 1.5 %fusion.134 = f32[19,8,32,128]{3,2,1,0:T(8,128)} fusion(f32[19,8,32,128]{3,2,1,0:T(8,128)} %fusion.133, f32[1,1,32,128]{3,2,1,0:T(8,128)} %slice_bitcast_fusion.33, f32[1,7,32,128]{3,2,1,0:T(8,128)S(1)} %slice_bitcast_fusion.14, f32[32,128]{1,0:T(8,128)} %get-tuple-element.134, pred[8]{0:T(512)(128)(4,1)} %copy-done.5), kind=kLoop, calls=%fused_computation.199 | loop fusion | flops 65536 | bytes 279040
  89.6 1.5 %fusion.135 = f32[19,8,32,128]{3,2,1,0:T(8,128)} fusion(f32[19,8,32,128]{3,2,1,0:T(8,128)} %fusion.134, f32[1,7,32,128]{3,2,1,0:T(8,128)S(1)} %slice_bitcast_fusion.13, f32[1,1,32,128]{3,2,1,0:T(8,128)} %slice_bitcast_fusion.39, f32[32,128]{1,0:T(8,128)S(1)} %get-tuple-element.129, pred[8]{0:T(512)(128)(4,1)} %copy-done.4), kind=kLoop, calls=%fused_computation.201 | loop fusion | flops 65536 | bytes 279040 | tf_op jit(solution)/shard_map/stack | solution.py:133
  91.7 5.5 %all-to-all-done.1 = f32[64,2,384]{2,1,0:T(2,128)S(1)} async-done(((f32[64,2,384]{2,1,0:T(2,128)}), f32[64,2,384]{2,1,0:T(2,128)S(1)}, u32[]{:S(2)}, u32[]{:S(2)}) %all-to-all-start.1) | async-done | bytes 196640 | tf_op jit(solution)/shard_map/all_to_all | solution.py:191
  97.4 1.0 convolution_convert_fusion
  98.4 1.2 %fusion.139 = f32[64,3,128]{2,1,0:T(4,128)S(1)} fusion(bf16[64,128,128]{2,1,0:T(8,128)(2,1)S(1)} %copy-done, bf16[64,3,128]{2,0,1:T(8,128)(2,1)S(1)} %convolution_convert_fusion), kind=kOutput, calls=%fused_computation.265 | convolution fusion | flops 6291456 | bytes 2244608 | tf_op jit(solution)/shard_map/bks,bcs->bkc/dot_general | solution.py:202
  (161 shorter events, 23.1 us)
Async XLA Ops:
  0.6 13.5 %copy-start = (bf16[64,128,128]{2,1,0:T(8,128)(2,1)S(1)}, bf16[64,128,128]{2,1,0:T(8,128)(2,1)}, u32[]{:S(2)}) copy-start(bf16[64,128,128]{2,1,0:T(8,128)(2,1)} %param.11) | copy-start | bytes 6291460
  4.5 11.4 %copy-start.7 = (s32[64]{0:T(128)}, s32[64]{0:T(128)S(1)}, u32[]{:S(2)}) copy-start(s32[64]{0:T(128)S(1)} %convert_add_fusion) | copy-start | bytes 772
  8.6 1.8 %copy-start.6 = (f32[4,19]{1,0:T(4,128)S(1)}, f32[4,19]{1,0:T(4,128)}, u32[]{:S(2)}) copy-start(f32[4,19]{1,0:T(4,128)} %constant.85.clone) | copy-start | bytes 916
  14.2 2.0 %copy-start.3 = (f32[64,2,1]{2,0,1:T(8,128)S(1)}, f32[64,2,1]{2,0,1:T(8,128)}, u32[]{:S(2)}) copy-start(f32[64,2,1]{2,0,1:T(8,128)} %copy.1883) | copy-start | bytes 1540
  17.1 55.7 %all-to-all-start = ((f32[64,2,385]{2,1,0:T(2,128)}), f32[64,2,385]{2,1,0:T(2,128)S(1)}, u32[]{:S(2)}, u32[]{:S(2)}) async-start(f32[64,2,385]{2,1,0:T(2,128)} %copy.1884), calls=%async_computation | async-start | bytes 524288 | tf_op jit(solution)/shard_map/all_to_all | solution.py:45
  27.5 3.3 %copy-start.1 = (f32[19,8,32,128]{3,2,1,0:T(8,128)S(1)}, f32[19,8,32,128]{3,2,1,0:T(8,128)}, u32[]{:S(2)}) copy-start(f32[19,8,32,128]{3,2,1,0:T(8,128)} %param.10) | copy-start | bytes 7471108
  32.4 7.4 %collective-permute-start.1 = (f32[5,8,32,1]{2,1,3,0:T(8,128)S(1)}, f32[5,8,32,1]{2,1,3,0:T(8,128)S(1)}, u32[]{:S(2)}, u32[]{:S(2)}) collective-permute-start(f32[5,8,32,1]{2,1,3,0:T(8,128)S(1)} %constant_dynamic-update-slice_fusion.5), channel_id=1, source_target_pairs={{0,192},{64,0},{128,64},{192,128},{1,193},{65,1},{129,65},{193,129... | collective-permute-start | bytes 15368 | tf_op jit(solution)/shard_map/ppermute | solution.py:37
  37.8 5.2 %collective-permute-start = (f32[5,8,32,1]{2,1,3,0:T(8,128)S(1)}, f32[5,8,32,1]{2,1,3,0:T(8,128)S(1)}, u32[]{:S(2)}, u32[]{:S(2)}) collective-permute-start(f32[5,8,32,1]{2,1,3,0:T(8,128)S(1)} %constant_dynamic-update-slice_fusion), channel_id=1, source_target_pairs={{0,64},{64,128},{128,192},{192,0},{1,65},{65,129},{129,193},{193,1... | collective-permute-start | bytes 15368 | tf_op jit(solution)/shard_map/ppermute | solution.py:37
  38.1 33.2 %copy-start.4 = (pred[8]{0:T(512)(128)(4,1)}, pred[8]{0:T(512)(128)(4,1)S(1)}, u32[]{:S(2)}) copy-start(pred[8]{0:T(512)(128)(4,1)S(1)} %iota_compare_fusion.7) | copy-start | bytes 28
  38.1 34.0 %copy-start.5 = (pred[8]{0:T(512)(128)(4,1)}, pred[8]{0:T(512)(128)(4,1)S(1)}, u32[]{:S(2)}) copy-start(pred[8]{0:T(512)(128)(4,1)S(1)} %iota_compare_fusion.6) | copy-start | bytes 28
  43.6 7.2 %collective-permute-start.2 = (f32[5,8,1,128]{3,1,2,0:T(8,128)S(1)}, f32[5,8,1,128]{3,1,2,0:T(8,128)S(1)}, u32[]{:S(2)}, u32[]{:S(2)}) collective-permute-start(f32[5,8,1,128]{3,1,2,0:T(8,128)S(1)} %constant_dynamic-update-slice_fusion.10), channel_id=1, source_target_pairs={{0,16},{16,32},{32,48},{48,0},{1,17},{17,33},{33,49},{49,1},{2,18}... | collective-permute-start | bytes 61448 | tf_op jit(solution)/shard_map/ppermute | solution.py:37
  46.8 3.3 %collective-permute-start.3 = (f32[5,8,1,128]{3,1,2,0:T(8,128)S(1)}, f32[5,8,1,128]{3,1,2,0:T(8,128)S(1)}, u32[]{:S(2)}, u32[]{:S(2)}) collective-permute-start(f32[5,8,1,128]{3,1,2,0:T(8,128)S(1)} %constant_dynamic-update-slice_fusion.15), channel_id=1, source_target_pairs={{0,48},{16,0},{32,16},{48,32},{1,49},{17,1},{33,17},{49,33},{2,50}... | collective-permute-start | bytes 61448 | tf_op jit(solution)/shard_map/ppermute | solution.py:37
  51.6 12.5 %collective-permute-start.5 = (f32[5,1,32,128]{3,2,1,0:T(8,128)S(1)}, f32[5,1,32,128]{3,2,1,0:T(8,128)S(1)}, u32[]{:S(2)}, u32[]{:S(2)}) collective-permute-start(f32[5,1,32,128]{3,2,1,0:T(8,128)S(1)} %constant_dynamic-update-slice_fusion.25), channel_id=1, source_target_pairs={{0,15},{1,0},{2,1},{3,2},{4,3},{5,4},{6,5},{7,6},{8,7},{9,8},{10,9... | collective-permute-start | bytes 245768 | tf_op jit(solution)/shard_map/ppermute | solution.py:37
  56.3 7.1 %collective-permute-start.4 = (f32[5,1,32,128]{3,2,1,0:T(8,128)S(1)}, f32[5,1,32,128]{3,2,1,0:T(8,128)S(1)}, u32[]{:S(2)}, u32[]{:S(2)}) collective-permute-start(f32[5,1,32,128]{3,2,1,0:T(8,128)S(1)} %constant_dynamic-update-slice_fusion.20), channel_id=1, source_target_pairs={{0,1},{1,2},{2,3},{3,4},{4,5},{5,6},{6,7},{7,8},{8,9},{9,10},{10,1... | collective-permute-start | bytes 245768 | tf_op jit(solution)/shard_map/ppermute | solution.py:37
  57.7 17.7 %copy-start.2 = (f32[8,128,128]{2,1,0:T(8,128)S(1)}, f32[8,128,128]{2,1,0:T(8,128)}, u32[]{:S(2)}) copy-start(f32[8,128,128]{2,1,0:T(8,128)} %param.14) | copy-start | bytes 1572868
  73.5 8.2 %collective-permute-start.6 = (f32[3,128]{1,0:T(4,128)S(1)}, f32[3,128]{1,0:T(4,128)S(1)}, u32[]{:S(2)}, u32[]{:S(2)}) collective-permute-start(f32[3,128]{1,0:T(4,128)S(1)} %bitcast.340), channel_id=1, source_target_pairs={{0,1},{1,2},{2,3},{3,4},{4,5},{5,6},{6,7},{7,8},{8,9},{9,10},{10,1... | collective-permute-start | bytes 4616 | tf_op jit(solution)/shard_map/ppermute | solution.py:55
  83.9 13.3 %all-to-all-start.1 = ((f32[64,2,384]{2,1,0:T(2,128)}), f32[64,2,384]{2,1,0:T(2,128)S(1)}, u32[]{:S(2)}, u32[]{:S(2)}) async-start(f32[64,2,384]{2,1,0:T(2,128)} %copy.1887), calls=%async_computation.1 | async-start | bytes 393216 | tf_op jit(solution)/shard_map/all_to_all | solution.py:191
where the time goes:
time: 101 us; the launch traced here: 100 us
  starting transfers between devices  29.9 us (30%)
  other arithmetic  24.8 us (25%)
  waiting for transfers between devices  21.2 us (21%)
  local copies, waits for them, and re-layouts  14.2 us (14%)
  matrix products  8.65 us (9%)
  between operations  1.57 us (2%)
    ppermute x6, starting transfers between devices, from_behind(): return lax.ppermute(value, axis, pairs)  13.4 us
    unnamed x18, other arithmetic  13.3 us
    all_to_all x1, starting transfers between devices, in_one_piece(): lax.all_to_all(both, axis, split_axis=split_dim, concat_axis=concat_dim,...  10.3 us
    ppermute x6, waiting for transfers between devices, from_behind(): return lax.ppermute(value, axis, pairs)  10 us
    ppermute x1, waiting for transfers between devices, from_behind_2(): return lax.ppermute(array, axis, pairs)  5.67 us
    all_to_all x1, waiting for transfers between devices, body(): lax.all_to_all(returned.reshape(owner_count, capacity, 3 * node_count), (...  5.49 us
    unnamed x42, local copies, waits for them, and re-layouts  5.2 us
    all_to_all x1, starting transfers between devices, body(): lax.all_to_all(returned.reshape(owner_count, capacity, 3 * node_count), (...  4.23 us
  transfers between devices with their start and end apart: 9, of which 5 were waited for; matrix products, arithmetic and copies ran while one was open for 25% of the time, Pallas kernels for 0%

commit v1 on v0

v1 whole, which is shorter than its diff:
```python
import jax
import jax.numpy as jnp
from jax import lax
from jax.experimental import pallas as pl
from jax.experimental.pallas import tpu as pltpu
from jax.sharding import PartitionSpec as P


lattice_velocity = (
    (0, 0, 0),
    (1, 0, 0),
    (-1, 0, 0),
    (0, 1, 0),
    (0, -1, 0),
    (0, 0, 1),
    (0, 0, -1),
    (1, 1, 0),
    (-1, -1, 0),
    (1, -1, 0),
    (-1, 1, 0),
    (1, 0, 1),
    (-1, 0, -1),
    (1, 0, -1),
    (-1, 0, 1),
    (0, 1, 1),
    (0, -1, -1),
    (0, 1, -1),
    (0, -1, 1),
)
lattice_weight = (1.0 / 3.0,) + (1.0 / 18.0,) * 6 + (1.0 / 36.0,) * 12
load_scale = 30.0
relaxation = 1.6

CZ, CY, CX = 8, 32, 128
ROWS = CZ * CY
NB, SB, SN = 64, 8, 128
OWNERS = 64
NEAR_BLOCKS = 16
OUT_ROWS = 10
BACK_ROWS = 7

VMEM = pl.BlockSpec(memory_space=pltpu.VMEM)
SMEM = pl.BlockSpec(memory_space=pltpu.SMEM)
ANY = pl.BlockSpec(memory_space=pl.ANY)


def moved(component, sign):
    return [d for d in range(19) if lattice_velocity[d][component] == sign]


XP, XM = moved(0, 1), moved(0, -1)
YP, YM = moved(1, 1), moved(1, -1)
ZP, ZM = moved(2, 1), moved(2, -1)
MOVING = XP + XM
STILL = moved(0, 0)
TURNED = [d for d in STILL if lattice_velocity[d][1] != 0]
BENT = [d for d in MOVING if lattice_velocity[d][1] != 0]
DIAGONAL = [d for d in TURNED if lattice_velocity[d][2] != 0]


def signed_sum(values, component):
    total = None
    for d in range(19):
        c = lattice_velocity[d][component]
        if c == 0:
            continue
        if total is None:
            total = values[d]
        elif c > 0:
            total = total + values[d]
        else:
            total = total - values[d]
    return total


def shape(dims, dtype=jnp.float32):
    return jax.ShapeDtypeStruct(dims, dtype)


def near(dims):
    return pltpu.VMEM(dims, jnp.float32)


def held(value):
    return pltpu.with_memory_space_constraint(value, pltpu.VMEM)


def far(value):
    return pltpu.with_memory_space_constraint(value, pltpu.HBM)


def cost(flops, moved_bytes):
    return pl.CostEstimate(flops=flops, bytes_accessed=moved_bytes, transcendentals=0)


def forces_body(
    row_hbm, owner_hbm, slot_hbm, pop_hbm, w_hbm, out_ref,
    row_s, owner_s, slot_s, pop, w, mom, seen, pop_sem, w_sem, in_sem,
):
    parts = 4
    integers = [
        pltpu.make_async_copy(a, b, in_sem.at[i])
        for i, (a, b) in enumerate(((row_hbm, row_s), (owner_hbm, owner_s), (slot_hbm, slot_s)))
    ]
    pop_copies = []
    for c in range(parts):
        rows = pl.ds(c * (ROWS // parts), ROWS // parts)
        pop_copies.append(
            pltpu.make_async_copy(pop_hbm.at[:, rows], pop.at[:, rows], pop_sem.at[c])
        )
    w_copies = []
    for c in range(parts):
        blocks = pl.ds(c * (NB // parts), NB // parts)
        w_copies.append(pltpu.make_async_copy(w_hbm.at[blocks], w.at[blocks], w_sem.at[c]))
    for copy in pop_copies + integers + w_copies:
        copy.start()
    out_ref[...] = jnp.zeros(out_ref.shape, jnp.float32)
    for o in range(OWNERS):
        seen[o] = 0
    for c in range(parts):
        pop_copies[c].wait()
        for t in range(c * (ROWS // parts // 8), (c + 1) * (ROWS // parts // 8)):
            values = [pop[d, t * 8 : t * 8 + 8, :] for d in range(19)]
            for k in range(3):
                mom[pl.ds(t * 64 + k, 8, stride=8), :] = load_scale * signed_sum(values, k)
    lane = lax.broadcasted_iota(jnp.int32, (1, 128), 1)
    for copy in integers:
        copy.wait()
    for b in range(NB):
        if b % (NB // parts) == 0:
            w_copies[b // (NB // parts)].wait()
        traction = mom[pl.ds(pl.multiple_of(row_s[b] * 8, 8), 8), :].astype(jnp.bfloat16)
        force = jnp.dot(traction, w[b], preferred_element_type=jnp.float32)[:3]
        owner = owner_s[b]
        rank = seen[owner]
        seen[owner] = rank + 1
        slot = slot_s[b]
        start = owner * OUT_ROWS
        out_ref[pl.ds(start + rank * 3, 3), :] = force
        pltpu.store(
            out_ref.at[pl.ds(start + 9, 1), :],
            jnp.full((1, 128), (slot + 1).astype(jnp.float32)),
            mask=lane == rank,
        )
        shared = jnp.logical_and(slot == SB - 1, owner < OWNERS - 1)
        after = jnp.where(owner < OWNERS - 1, owner + 1, 0) * OUT_ROWS + 6
        out_ref[pl.ds(after, 3), :] += jnp.where(shared, force, 0.0)


def send_forces(rows, owners, slots, populations, weights):
    return pl.pallas_call(
        forces_body,
        out_shape=near((OWNERS * OUT_ROWS, 128)),
        in_specs=[ANY] * 5,
        out_specs=VMEM,
        scratch_shapes=[
            pltpu.SMEM((NB,), jnp.int32),
            pltpu.SMEM((NB,), jnp.int32),
            pltpu.SMEM((NB,), jnp.int32),
            pltpu.VMEM((19, ROWS, CX), jnp.float32),
            pltpu.VMEM((NB, CX, SN), jnp.bfloat16),
            pltpu.VMEM((ROWS * 8, CX), jnp.float32),
            pltpu.SMEM((OWNERS,), jnp.int32),
            pltpu.SemaphoreType.DMA((4,)),
            pltpu.SemaphoreType.DMA((4,)),
            pltpu.SemaphoreType.DMA((3,)),
        ],
        cost_estimate=cost(50_000_000, 5_000_000),
        compiler_params=pltpu.CompilerParams(vmem_limit_bytes=16 * 1024 * 1024),
        name="forces",
    )(far(rows), far(owners), far(slots), far(populations), far(weights))


def two_parts(x):
    high = x.astype(jnp.bfloat16)
    return high, (x - high.astype(jnp.float32)).astype(jnp.bfloat16)


def owner_body(in_ref, comp_hbm, near_hbm, yz_ref, disp_ref, back_ref, comp, left, right, sem):
    copies = [pltpu.make_async_copy(near_hbm, comp.at[SB], sem.at[SB])]
    for s in range(SB):
        copies.append(pltpu.make_async_copy(comp_hbm.at[s], comp.at[s], sem.at[s]))
    for copy in copies:
        copy.start()

    b, e = lax.axis_index("gy"), lax.axis_index("gz")
    for j, d in enumerate(DIAGONAL):
        _, cy, cz = lattice_velocity[d]
        chunk = lax.rem(b + cy + 4, 4) * 16 + lax.rem(e + cz + 16, 16)
        back_ref[pl.ds(chunk * BACK_ROWS + 6, 1), :] = yz_ref[j : j + 1, :]

    def rows_of(j):
        return in_ref[pl.ds(j, OWNERS, stride=OUT_ROWS), :]

    def mm(a, b):
        return jnp.dot(a, b, preferred_element_type=jnp.float32)

    tags = rows_of(9)
    lane = lax.broadcasted_iota(jnp.int32, (OWNERS, 128), 1).astype(jnp.float32) + 1.0
    chosen = jnp.concatenate(
        [
            (jnp.broadcast_to(tags[:, r : r + 1], (OWNERS, 128)) == lane).astype(jnp.float32)
            for r in range(2)
        ],
        axis=0,
    )
    select = chosen.T[:SB].astype(jnp.bfloat16)
    left[...] = jnp.zeros(left.shape, jnp.float32)
    for k in range(3):
        arrived = jnp.concatenate([rows_of(k), rows_of(3 + k)], axis=0)
        high, low = two_parts(arrived)
        loads = mm(select, high) + mm(select, low)
        high, low = two_parts(loads)
        left[pl.ds(k, SB, stride=8), :] = high.astype(jnp.float32)
        left[pl.ds(3 + k, SB, stride=8), :] = low.astype(jnp.float32)
        shared = jnp.sum(rows_of(6 + k), axis=0, keepdims=True)
        high, low = two_parts(shared)
        left[SB * 8 + k : SB * 8 + k + 1, :] = high.astype(jnp.float32)
        left[SB * 8 + 3 + k : SB * 8 + 4 + k, :] = low.astype(jnp.float32)

    def product(s, matrix):
        high, low = two_parts(matrix)
        rows = left[s * 8 : s * 8 + 8, :].astype(jnp.bfloat16)
        first = mm(rows, high)
        return first[:3] + first[3:6] + mm(rows, low)[:3]

    copies[0].wait()
    for s in range(SB):
        copies[1 + s].wait()
        moved_by = product(s, comp[s])
        if s == 0:
            moved_by = moved_by + product(SB, comp[SB])
        disp_ref[:, s, :] = moved_by
        right[s * 8 : s * 8 + 3, :] = moved_by
    chosen = chosen.astype(jnp.bfloat16)
    for k in range(3):
        nodes = right[pl.ds(k, SB, stride=8), :].astype(jnp.bfloat16).astype(jnp.float32)
        nodes = jnp.concatenate([nodes, jnp.zeros((128 - SB, 128), jnp.float32)], axis=0)
        back = mm(chosen, nodes.astype(jnp.bfloat16))
        for r in range(2):
            back_ref[pl.ds(3 * r + k, OWNERS, stride=BACK_ROWS), :] = back[
                r * OWNERS : (r + 1) * OWNERS
            ]


def owner_step(arrived, compliance, neighbour, lines):
    return pl.pallas_call(
        owner_body,
        out_shape=(shape((3, SB, SN)), near((OWNERS * BACK_ROWS, 128))),
        in_specs=[VMEM, ANY, ANY, VMEM],
        out_specs=(VMEM, VMEM),
        scratch_shapes=[
            pltpu.VMEM((SB + 1, SN, SN), jnp.float32),
            pltpu.VMEM((SB * 8 + 8, 128), jnp.float32),
            pltpu.VMEM((SB * 8, 128), jnp.float32),
            pltpu.SemaphoreType.DMA((SB + 1,)),
        ],
        cost_estimate=cost(20_000_000, 1_200_000),
        compiler_params=pltpu.CompilerParams(vmem_limit_bytes=16 * 1024 * 1024),
        name="owner",
    )(held(arrived), far(compliance), far(neighbour), held(lines))


def wall_body(owner_hbm, in_ref, w_near, w_hbm, out_ref, owner_s, w, seen, w_sem, in_sem):
    owner_copy = pltpu.make_async_copy(owner_hbm, owner_s, in_sem)
    owner_copy.start()
    parts = 6
    size = (NB - NEAR_BLOCKS) // parts
    w_copies = []
    for c in range(parts):
        w_copies.append(
            pltpu.make_async_copy(
                w_hbm.at[pl.ds(NEAR_BLOCKS + c * size, size)], w.at[pl.ds(c * size, size)], w_sem.at[c]
            )
        )
    for copy in w_copies:
        copy.start()
    for o in range(OWNERS):
        seen[o] = 0
    owner_copy.wait()
    for b in range(NB):
        if b < NEAR_BLOCKS:
            weight = w_near[b]
        else:
            if (b - NEAR_BLOCKS) % size == 0:
                w_copies[(b - NEAR_BLOCKS) // size].wait()
            weight = w[b - NEAR_BLOCKS]
        owner = owner_s[b]
        rank = seen[owner]
        seen[owner] = rank + 1
        nodes = in_ref[pl.ds(owner * BACK_ROWS + rank * 3, 3), :].astype(jnp.bfloat16)
        out_ref[:, b, :] = lax.dot_general(
            nodes, weight, (((1,), (1,)), ((), ())), preferred_element_type=jnp.float32
        )


def wall_step(owners, arrived, first_weights, weights):
    return pl.pallas_call(
        wall_body,
        out_shape=shape((3, NB, CX)),
        in_specs=[ANY, VMEM, VMEM, ANY],
        out_specs=VMEM,
        scratch_shapes=[
            pltpu.SMEM((NB,), jnp.int32),
            pltpu.VMEM((NB - NEAR_BLOCKS, CX, SN), jnp.bfloat16),
            pltpu.SMEM((OWNERS,), jnp.int32),
            pltpu.SemaphoreType.DMA((6,)),
            pltpu.SemaphoreType.DMA,
        ],
        cost_estimate=cost(20_000_000, 2_500_000),
        compiler_params=pltpu.CompilerParams(vmem_limit_bytes=16 * 1024 * 1024),
        name="wall",
    )(far(owners), held(arrived), held(first_weights), far(weights))


def collide_body(
    pop_hbm,
    new_hbm,
    rel_ref,
    xp_ref,
    xm_ref,
    yp_ref,
    ym_ref,
    zp_ref,
    zm_ref,
    edge_ref,
    yz_ref,
    pop,
    packed,
    still,
    turned_to,
    sem,
    pop_sem,
):
    arriving = [
        pltpu.make_async_copy(pop_hbm.at[:, z], pop.at[:, z], pop_sem.at[z]) for z in range(CZ)
    ]
    for copy in arriving:
        copy.start()
    lane = lax.broadcasted_iota(jnp.int32, (8, 128), 1)
    for z in range(CZ):
        arriving[z].wait()
        for t in range(CY // 8):
            rows = pl.ds(t * 8, 8)
            f = [pop[d, z, rows, :] for d in range(19)]
            density = f[0]
            for d in range(1, 19):
                density = density + f[d]
            inverse = 1.0 / density
            v = [signed_sum(f, k) * inverse for k in range(3)]
            speed_square = v[0] * v[0] + v[1] * v[1] + v[2] * v[2]
            base = 1.0 - 1.5 * speed_square
            weighted = {w: (relaxation * w) * density for w in set(lattice_weight)}
            pack = jnp.zeros((8, 128), jnp.float32)
            for d in range(19):
                c = lattice_velocity[d]
                projected = None
                for k in range(3):
                    if c[k] != 0:
                        term = v[k] if c[k] > 0 else -v[k]
                        projected = term if projected is None else projected + term
                bracket = base
                if projected is not None:
                    bracket = bracket + projected * (3.0 + 4.5 * projected)
                value = (1.0 - relaxation) * f[d] + weighted[lattice_weight[d]] * bracket
                if c[0] > 0:
                    i = XP.index(d)
                    value = pltpu.roll(value, 1, 1)
                    edge = value if i == 0 else pltpu.roll(value, i, 1)
                    pack = jnp.where(lane == i, edge, pack)
                elif c[0] < 0:
                    i = 8 + XM.index(d)
                    value = pltpu.roll(value, 127, 1)
                    pack = jnp.where(lane == i, pltpu.roll(value, i + 1, 1), pack)
                if c[0] != 0:
                    rel_ref[MOVING.index(d), z, rows, :] = value
                else:
                    still[STILL.index(d), z, rows, :] = value
            packed[pl.ds(z * CY + t * 8, 8), :] = pack

    for h in range(2):
        turned = packed[h * 128 : h * 128 + 128, :].T
        xp_ref[:, h * 128 : h * 128 + 128] = turned[0:8]
        xm_ref[:, h * 128 : h * 128 + 128] = turned[8:16]

    copies = []
    for i, d in enumerate(STILL):
        _, cy, cz = lattice_velocity[d]
        first, count = (1, CZ - 1) if cz > 0 else (0, CZ - 1) if cz < 0 else (0, CZ)
        if cy == 0:
            source = still.at[i, pl.ds(first - cz, count)]
        else:
            spread(
                d, lambda z: still[i, z], turned_to.at[i], edge_ref.at[TURNED.index(d)],
                yp_ref, ym_ref, zp_ref, zm_ref,
            )
            source = turned_to.at[i, pl.ds(first, count)]
        if d in DIAGONAL:
            at = CZ - 1 if cz > 0 else 0
            line = CY - 1 if cy > 0 else 0
            j = DIAGONAL.index(d)
            yz_ref[j : j + 1, :] = still[i, at, line : line + 1, :]
        copy = pltpu.make_async_copy(source, new_hbm.at[d, pl.ds(first, count)], sem.at[i])
        copy.start()
        copies.append(copy)
    zp_ref[ZP.index(5)] = still[STILL.index(5), CZ - 1]
    zm_ref[ZM.index(6)] = still[STILL.index(6), 0]
    for copy in copies:
        copy.wait()


def spread(d, plane_of, res, edge, yp_ref, ym_ref, zp_ref, zm_ref):
    _, cy, cz = lattice_velocity[d]
    for z in range(CZ):
        value = plane_of(z)
        if cy > 0:
            yp_ref[z, YP.index(d) : YP.index(d) + 1, :] = value[CY - 1 : CY]
            value = pltpu.roll(value, 1, 0)
        elif cy < 0:
            ym_ref[z, YM.index(d) : YM.index(d) + 1, :] = value[0:1]
            value = pltpu.roll(value, CY - 1, 0)
        if 0 <= z + cz < CZ:
            res[z + cz] = value
            if cy > 0:
                edge[z + cz] = value[:8]
            elif cy < 0:
                edge[z + cz] = value[CY - 8 :]
        elif cz > 0:
            zp_ref[ZP.index(d)] = value
        else:
            zm_ref[ZM.index(d)] = value


def collide_step(populations):
    return pl.pallas_call(
        collide_body,
        out_shape=(
            shape((19, CZ, CY, CX)),
            near((10, CZ, CY, CX)),
            near((8, ROWS)),
            near((8, ROWS)),
            near((CZ, 8, CX)),
            near((CZ, 8, CX)),
            near((5, CY, CX)),
            near((5, CY, CX)),
            near((6, CZ, 8, CX)),
            near((8, CX)),
        ),
        in_specs=[ANY],
        out_specs=(ANY,) + (VMEM,) * 9,
        scratch_shapes=[
            pltpu.VMEM((19, CZ, CY, CX), jnp.float32),
            pltpu.VMEM((ROWS, 128), jnp.float32),
            pltpu.VMEM((9, CZ, CY, CX), jnp.float32),
            pltpu.VMEM((9, CZ, CY, CX), jnp.float32),
            pltpu.SemaphoreType.DMA((9,)),
            pltpu.SemaphoreType.DMA((CZ,)),
        ],
        cost_estimate=cost(10_000_000, 5_000_000),
        compiler_params=pltpu.CompilerParams(vmem_limit_bytes=16 * 1024 * 1024),
        name="collide",
    )(far(populations))


def stream_body(
    new_in,
    w_hbm,
    rel,
    lo_ref,
    hi_ref,
    yp_in,
    ym_in,
    zp_in,
    zm_in,
    new_hbm,
    yp_ref,
    ym_ref,
    zp_ref,
    zm_ref,
    edge_ref,
    w_ref,
    res,
    cols,
    sem,
    w_sem,
):
    w_copy = pltpu.make_async_copy(w_hbm.at[pl.ds(0, NEAR_BLOCKS)], w_ref, w_sem)
    w_copy.start()
    yp_ref[...] = yp_in[...]
    ym_ref[...] = ym_in[...]
    zp_ref[...] = zp_in[...]
    zm_ref[...] = zm_in[...]
    pad = jnp.zeros((120, 128), jnp.float32)
    for h in range(2):
        for side, ref in enumerate((lo_ref, hi_ref)):
            block = jnp.concatenate([ref[:, h * 128 : h * 128 + 128], pad], axis=0)
            cols[side, h * 128 : h * 128 + 128, :] = block.T
    lane = lax.broadcasted_iota(jnp.int32, (CY, CX), 1)
    copies = []
    for j, d in enumerate(MOVING):
        cx, cy, cz = lattice_velocity[d]
        side, i, at = (0, j, 0) if cx > 0 else (1, j - 5, CX - 1)

        def plane(z):
            column = jnp.broadcast_to(cols[side, z * CY : (z + 1) * CY, i : i + 1], (CY, CX))
            return jnp.where(lane == at, column, rel[j, z])

        edge = edge_ref.at[BENT.index(d)] if cy != 0 else None
        spread(d, plane, res.at[j], edge, yp_ref, ym_ref, zp_ref, zm_ref)
        first, count = (1, CZ - 1) if cz > 0 else (0, CZ - 1) if cz < 0 else (0, CZ)
        planes = pl.ds(first, count)
        copy = pltpu.make_async_copy(res.at[j, planes], new_hbm.at[d, planes], sem.at[j])
        copy.start()
        copies.append(copy)
    w_copy.wait()
    for copy in copies:
        copy.wait()


def stream_step(new, weights, moving, below, above, faces):
    return pl.pallas_call(
        stream_body,
        out_shape=(
            shape((19, CZ, CY, CX)),
            near((CZ, 8, CX)),
            near((CZ, 8, CX)),
            near((5, CY, CX)),
            near((5, CY, CX)),
            near((4, CZ, 8, CX)),
            pltpu.VMEM((NEAR_BLOCKS, CX, SN), jnp.bfloat16),
        ),
        in_specs=[ANY] * 2 + [VMEM] * 7,
        out_specs=(ANY,) + (VMEM,) * 6,
        input_output_aliases={0: 0},
        scratch_shapes=[
            pltpu.VMEM((10, CZ, CY, CX), jnp.float32),
            pltpu.VMEM((2, ROWS, 128), jnp.float32),
            pltpu.SemaphoreType.DMA((10,)),
            pltpu.SemaphoreType.DMA,
        ],
        cost_estimate=cost(10_000_000, 5_000_000),
        compiler_params=pltpu.CompilerParams(vmem_limit_bytes=16 * 1024 * 1024),
        name="stream",
    )(new, far(weights), held(moving), held(below), held(above), *[held(f) for f in faces])


def finish_body(
    new_in, still_ref, moving_ref, ylo, yhi, zlo, zhi, back_ref, new_hbm, tiles, planes, sem
):
    b, e = lax.axis_index("gy"), lax.axis_index("gz")
    copies = []

    def send(source, target):
        copy = pltpu.make_async_copy(source, target, sem.at[len(copies)])
        copy.start()
        copies.append(copy)

    for sign, dirs, halo, at in ((1, ZP, zlo, 0), (-1, ZM, zhi, CZ - 1)):
        for j, d in enumerate(dirs):
            if d in DIAGONAL:
                cy = lattice_velocity[d][1]
                chunk = lax.rem(b - cy + 4, 4) * 16 + lax.rem(e - sign + 16, 16)
                slot = DIAGONAL.index(d)
                line = 0 if cy > 0 else CY - 1
                planes[slot] = halo[j]
                planes[slot, line : line + 1, :] = back_ref[pl.ds(chunk * BACK_ROWS + 6, 1), :]
                send(planes.at[slot], new_hbm.at[d, at])
            else:
                send(halo.at[j], new_hbm.at[d, at])
    for j, d in enumerate(YP + YM):
        cx, cy, cz = lattice_velocity[d]
        ref, i, at = (ylo, j, 0) if cy > 0 else (yhi, j - 5, CY - 1)
        edge = still_ref.at[TURNED.index(d)] if cx == 0 else moving_ref.at[BENT.index(d)]
        for z in range(CZ):
            if 0 <= z + cz < CZ:
                tiles[j, z + cz] = edge[z + cz]
                tiles[j, z + cz, at % 8 : at % 8 + 1, :] = ref[z, i : i + 1, :]
        first, count = (1, CZ - 1) if cz > 0 else (0, CZ - 1) if cz < 0 else (0, CZ)
        inside = pl.ds(first, count)
        send(tiles.at[j, inside], new_hbm.at[d, inside, pl.ds(at // 8 * 8, 8)])
    for copy in copies:
        copy.wait()


def finish_step(new, still, moving, ylo, yhi, zlo, zhi, back):
    return pl.pallas_call(
        finish_body,
        out_shape=shape((19, CZ, CY, CX)),
        in_specs=[ANY] + [VMEM] * 7,
        out_specs=ANY,
        input_output_aliases={0: 0},
        scratch_shapes=[
            pltpu.VMEM((10, CZ, 8, CX), jnp.float32),
            pltpu.VMEM((4, CY, CX), jnp.float32),
            pltpu.SemaphoreType.DMA((20,)),
        ],
        cost_estimate=cost(100_000, 1_000_000),
        compiler_params=pltpu.CompilerParams(vmem_limit_bytes=16 * 1024 * 1024),
        name="finish",
    )(new, *[held(x) for x in (still, moving, ylo, yhi, zlo, zhi, back)])


def from_behind(value, axis, steps):
    count = lax.axis_size(axis)
    pairs = [(source, (source + steps) % count) for source in range(count)]
    return lax.ppermute(value, axis, pairs)


def exchange(value):
    return lax.all_to_all(value, ("gy", "gz"), split_axis=0, concat_axis=0, tiled=True)


def body(
    populations, rbf_weights, owner_map, shell_slot, compliance, neighbour_compliance, interface_row
):
    owners = owner_map.reshape(NB)
    slots = shell_slot.reshape(NB)
    outgoing = send_forces(
        interface_row, owners, slots, populations.reshape(19, ROWS, CX), rbf_weights
    )
    incoming = exchange(outgoing.reshape(OWNERS, 1, OUT_ROWS * 128))
    new, relaxed, xp, xm, yp, ym, zp, zm, still, lines = collide_step(populations)
    xlo = from_behind(xp, "gx", 1)
    xhi = from_behind(xm, "gx", -1)
    displacement, back = owner_step(
        incoming.reshape(OWNERS * OUT_ROWS, 128), compliance, neighbour_compliance, lines
    )
    arrived = exchange(back.reshape(OWNERS, 1, BACK_ROWS * 128))
    new, yp, ym, zp, zm, bent, weights = stream_step(
        new, rbf_weights, relaxed, xlo, xhi, (yp, ym, zp, zm)
    )
    ylo = from_behind(yp, "gy", 1)
    yhi = from_behind(ym, "gy", -1)
    zlo = from_behind(zp, "gz", 1)
    zhi = from_behind(zm, "gz", -1)
    arrived = arrived.reshape(OWNERS * BACK_ROWS, 128)
    wall_motion = wall_step(owners, arrived, weights, rbf_weights)
    new = finish_step(new, still, bent, ylo, yhi, zlo, zhi, arrived)
    return (new, displacement.transpose(1, 0, 2), wall_motion.transpose(1, 0, 2))


def solution(mesh):
    return jax.shard_map(
        body,
        mesh=mesh,
        in_specs=(
            P(None, "gz", "gy", "gx"),
            P(("gx", "gy", "gz"), None, None),
            P(("gx", "gy", "gz"), None),
            P(("gx", "gy", "gz"), None),
            P(("gx", "gy", "gz"), None, None),
            P(("gx", "gy", "gz"), None),
            P(("gx", "gy", "gz")),
        ),
        out_specs=(
            P(None, "gz", "gy", "gx"),
            P(("gx", "gy", "gz"), None, None),
            P(("gx", "gy", "gz"), None, None),
        ),
        check_vma=False,
    )
```

time: 101 us -> 55.5 us (0.55)
  other arithmetic: 24.8 us -> 0 us
  Pallas kernels: 0 us -> 17.3 us
  local copies, waits for them, and re-layouts: 14.2 us -> 0 us
  waiting for transfers between devices: 21.2 us -> 8.67 us
  matrix products: 8.65 us -> 0 us
  starting transfers between devices: 29.9 us -> 28.4 us
    pallas_call x0 -> x6, Pallas kernels: none -> 17.3 us  [the longest x1 4.09 us: collide_step(): pl.pallas_call(collide_body, out_shape=(shape((19, CZ, CY, CX)), near((10...]
    unnamed x18 -> x0, other arithmetic: 13.3 us -> none
    dot_general x10 -> x0, matrix products: 8.65 us -> none  [the longest x1 1.75 us: collide(): jnp.dot(moment_matrix(), flattened, precision=lax.Precision.HIGHEST)]
    ppermute x6, waiting for transfers between devices: 10 us -> 3.04 us  [from_behind(): return lax.ppermute(value, axis, pairs)]
    ppermute x1 -> x0, waiting for transfers between devices: 5.67 us -> none  [from_behind_2(): return lax.ppermute(array, axis, pairs)]
    unnamed x42 -> x0, local copies, waits for them, and re-layouts: 5.2 us -> none
    sub x3 -> x0, other arithmetic: 3.27 us -> none  [collide(): flattened[direction] - relaxation * (flattened[direction] - equilibrium)]
    another operation x20 -> x0, local copies, waits for them, and re-layouts: 2.57 us -> none  [the longest x2 1.29 us: in_one_piece(): a.reshape(*a.shape[:along], w)]
  transfers between devices with their start and end apart: 9 -> 8, of which waited for: 5 -> 2; matrix products, arithmetic and copies ran while one was open for 25% -> 0% of each run, Pallas kernels for 0% -> 17%
where the time goes in v1:
time: 55.5 us; the launch traced here: 55.1 us
  starting transfers between devices  28.4 us (51%)
  Pallas kernels  17.3 us (31%)
  waiting for transfers between devices  8.67 us (16%)
  between operations  0.72 us (1%)
    all_to_all x2, starting transfers between devices, exchange(): lax.all_to_all(value, ('gy', 'gz'), split_axis=0, concat_axis=0, tiled=True)  15.7 us
    ppermute x6, starting transfers between devices, from_behind(): return lax.ppermute(value, axis, pairs)  12.7 us
    all_to_all x2, waiting for transfers between devices, exchange(): lax.all_to_all(value, ('gy', 'gz'), split_axis=0, concat_axis=0, tiled=True)  5.63 us
    pallas_call x1, Pallas kernels, collide_step(): pl.pallas_call(collide_body, out_shape=(shape((19, CZ, CY, CX)), near((10...  4.09 us
    pallas_call x1, Pallas kernels, send_forces(): pl.pallas_call(forces_body, out_shape=near((OWNERS * OUT_ROWS, 128)), in_...  4.05 us
    pallas_call x1, Pallas kernels, wall_step(): pl.pallas_call(wall_body, out_shape=shape((3, NB, CX)), in_specs=[ANY, VM...  3.41 us
    ppermute x6, waiting for transfers between devices, from_behind(): return lax.ppermute(value, axis, pairs)  3.04 us
    pallas_call x1, Pallas kernels, owner_step(): pl.pallas_call(owner_body, out_shape=(shape((3, SB, SN)), near((OWNERS *...  2.98 us
  transfers between devices with their start and end apart: 8, of which 2 were waited for; matrix products, arithmetic and copies ran while one was open for 0% of the time, Pallas kernels for 17%

profile of v1, /device:TPU:1, one launch (start us, length us, event | category | flops | bytes accessed | tf_op | source)
XLA Modules:
  0.0 55.1 jit_solution(15360942819828285752)
XLA Ops:
  0.6 4.0 %forces.1 = f32[640,128]{1,0:T(8,128)} custom-call(s32[64]{0:T(128)} %row_hbm.1, s32[64]{0:T(128)} %bitcast.14, s32[64]{0:T(128)} %bitcast.16, f32[19,256,128]{2,1,0:T(8,128)} %bitcast.12, bf16[64,128,128]{2,1,0:T(8,128)(2,1)} %w_hbm.5), custom_call_target="tpu_custom_call" | custom-call | flops 50000000 | bytes 5000000 | tf_op jit(solution)/shard_map/forces/pallas_call | solution.py:151
  4.7 10.4 %all-to-all-start = ((f32[64,1,1280]{2,1,0:T(1,128)}), f32[64,1,1280]{2,1,0:T(1,128)S(1)}, u32[]{:S(2)}, u32[]{:S(2)}) async-start(f32[64,1,1280]{2,1,0:T(1,128)} %bitcast.3), calls=%async_computation | async-start | bytes 655360 | tf_op jit(solution)/shard_map/all_to_all | solution.py:610
  15.0 4.1 %collide.1 = (f32[19,8,32,128]{3,2,1,0:T(8,128)}, f32[10,8,32,128]{3,2,1,0:T(8,128)S(1)}, f32[8,256]{1,0:T(8,128)S(1)}, f32[8,256]{1,0:T(8,128)S(1)}, f32[8,8,12...) custom-call(f32[19,8,32,128]{3,2,1,0:T(8,128)} %pop_hbm.1), custom_call_target="tpu_custom_call" | custom-call | flops 10000000 | bytes 5000000 | tf_op jit(solution)/shard_map/collide/pallas_call | solution.py:435
  19.1 5.6 %all-to-all-done = f32[64,1,1280]{2,1,0:T(1,128)S(1)} async-done(((f32[64,1,1280]{2,1,0:T(1,128)}), f32[64,1,1280]{2,1,0:T(1,128)S(1)}, u32[]{:S(2)}, u32[]{:S(2)}) %all-to-all-start) | async-done | bytes 327712 | tf_op jit(solution)/shard_map/all_to_all | solution.py:610
  24.8 3.0 %owner.1 = (f32[3,8,128]{2,1,0:T(8,128)}, f32[448,128]{1,0:T(8,128)}) custom-call(f32[640,128]{1,0:T(8,128)S(1)} %bitcast.11, f32[8,128,128]{2,1,0:T(8,128)} %comp_hbm.1, f32[128,128]{1,0:T(8,128)} %near_hbm.1, f32[8,128]{1,0:T(8,128)S(1)} %get-tuple-element.37.yz_ref), custom_call_target="tpu_custom_call" | custom-call | flops 20000000 | bytes 1200000 | tf_op jit(solution)/shard_map/owner/pallas_call | solution.py:247
  27.8 5.4 %all-to-all-start.1 = ((f32[64,1,896]{2,1,0:T(1,128)}), f32[64,1,896]{2,1,0:T(1,128)S(1)}, u32[]{:S(2)}, u32[]{:S(2)}) async-start(f32[64,1,896]{2,1,0:T(1,128)} %bitcast.5), calls=%async_computation.1 | async-start | bytes 458752 | tf_op jit(solution)/shard_map/all_to_all | solution.py:610
  33.1 3.1 %collective-permute-start = (f32[8,256]{1,0:T(8,128)S(1)}, f32[8,256]{1,0:T(8,128)S(1)}, u32[]{:S(2)}, u32[]{:S(2)}) collective-permute-start(f32[8,256]{1,0:T(8,128)S(1)} %get-tuple-element.24), channel_id=1, source_target_pairs={{0,64},{64,128},{128,192},{192,0},{1,65},{65,129},{129,193},{193,1... | collective-permute-start | bytes 24584 | tf_op jit(solution)/shard_map/ppermute | solution.py:606
  36.2 2.2 %collective-permute-start.1 = (f32[8,256]{1,0:T(8,128)S(1)}, f32[8,256]{1,0:T(8,128)S(1)}, u32[]{:S(2)}, u32[]{:S(2)}) collective-permute-start(f32[8,256]{1,0:T(8,128)S(1)} %get-tuple-element.25), channel_id=1, source_target_pairs={{0,192},{64,0},{128,64},{192,128},{1,193},{65,1},{129,65},{193,129... | collective-permute-start | bytes 24584 | tf_op jit(solution)/shard_map/ppermute | solution.py:606
  38.4 3.0 %collective-permute-done.lo_ref = f32[8,256]{1,0:T(8,128)S(1)} collective-permute-done((f32[8,256]{1,0:T(8,128)S(1)}, f32[8,256]{1,0:T(8,128)S(1)}, u32[]{:S(2)}, u32[]{:S(2)}) %collective-permute-start) | collective-permute-done | bytes 8224 | tf_op jit(solution)/shard_map/ppermute | solution.py:606
  41.4 0.0 collective-permute-done.1.hi_ref
  41.4 1.9 %stream.1 = (f32[19,8,32,128]{3,2,1,0:T(8,128)}, f32[8,8,128]{2,1,0:T(8,128)S(1)}, f32[8,8,128]{2,1,0:T(8,128)S(1)}, f32[5,32,128]{2,1,0:T(8,128)S(1)}, f32[5,32...) custom-call(f32[19,8,32,128]{3,2,1,0:T(8,128)} %get-tuple-element.22, ...), custom_call_target="tpu_custom_call", output_to_operand_aliasing={{0}: (0, {})} | custom-call | flops 10000000 | bytes 5000000 | tf_op jit(solution)/shard_map/stream/pallas_call | solution.py:521
  43.3 1.5 %collective-permute-start.4 = (f32[5,32,128]{2,1,0:T(8,128)S(1)}, f32[5,32,128]{2,1,0:T(8,128)S(1)}, u32[]{:S(2)}, u32[]{:S(2)}) collective-permute-start(f32[5,32,128]{2,1,0:T(8,128)S(1)} %get-tuple-element.35), channel_id=1, source_target_pairs={{0,1},{1,2},{2,3},{3,4},{4,5},{5,6},{6,7},{7,8},{8,9},{9,10},{10,1... | collective-permute-start | bytes 245768 | tf_op jit(solution)/shard_map/ppermute | solution.py:606
  44.8 3.4 %collective-permute-start.5 = (f32[5,32,128]{2,1,0:T(8,128)S(1)}, f32[5,32,128]{2,1,0:T(8,128)S(1)}, u32[]{:S(2)}, u32[]{:S(2)}) collective-permute-start(f32[5,32,128]{2,1,0:T(8,128)S(1)} %get-tuple-element.36), channel_id=1, source_target_pairs={{0,15},{1,0},{2,1},{3,2},{4,3},{5,4},{6,5},{7,6},{8,7},{9,8},{10,9... | collective-permute-start | bytes 245768 | tf_op jit(solution)/shard_map/ppermute | solution.py:606
  48.2 2.5 %collective-permute-start.2 = (f32[8,8,128]{2,1,0:T(8,128)S(1)}, f32[8,8,128]{2,1,0:T(8,128)S(1)}, u32[]{:S(2)}, u32[]{:S(2)}) collective-permute-start(f32[8,8,128]{2,1,0:T(8,128)S(1)} %get-tuple-element.33), channel_id=1, source_target_pairs={{0,16},{16,32},{32,48},{48,0},{1,17},{17,33},{33,49},{49,1},{2,18}... | collective-permute-start | bytes 98312 | tf_op jit(solution)/shard_map/ppermute | solution.py:606
  50.7 0.0 collective-permute-start.3
  50.7 0.0 all-to-all-done.1
  50.7 3.4 %wall.1 = f32[3,64,128]{2,1,0:T(8,128)} custom-call(s32[64]{0:T(128)} %bitcast.15, f32[448,128]{1,0:T(8,128)S(1)} %bitcast.9, bf16[16,128,128]{2,1,0:T(8,128)(2,1)S(1)} %get-tuple-element.40.w_near, bf16[64,128,128]{2,1,0:T(8,128)(2,1)} %w_hbm.5), custom_call_target="tpu_custom_call" | custom-call | flops 20000000 | bytes 2500000 | tf_op jit(solution)/shard_map/wall/pallas_call | solution.py:298
  54.2 0.0 collective-permute-done.2.ylo
  54.2 0.0 collective-permute-done.3.yhi
  54.2 0.0 collective-permute-done.4.zlo
  54.2 0.0 collective-permute-done.5.zhi
  54.2 0.9 %finish.1 = f32[19,8,32,128]{3,2,1,0:T(8,128)} custom-call(f32[19,8,32,128]{3,2,1,0:T(8,128)} %get-tuple-element.30.new_in, f32[6,8,8,128]{3,2,1,0:T(8,128)S(1)} %get-tuple-element.31.still_ref, f32[4,8,8,128]{3,2,1,0:T(8,128)S(1)} %get-tuple-element.32.moving_ref, f32[8,8,128]{2,1,0:T(8,128)S(1)} %collective-permute-done.2.ylo, ...), custom_call_target="tpu_custom_call", output_to_operand_aliasing={{}: (0, {})} | custom-call | flops 100000 | bytes 1000000 | tf_op jit(solution)/shard_map/finish/pallas_call | solution.py:586
Async XLA Ops:
  4.7 20.1 %all-to-all-start = ((f32[64,1,1280]{2,1,0:T(1,128)}), f32[64,1,1280]{2,1,0:T(1,128)S(1)}, u32[]{:S(2)}, u32[]{:S(2)}) async-start(f32[64,1,1280]{2,1,0:T(1,128)} %bitcast.3), calls=%async_computation | async-start | bytes 655360 | tf_op jit(solution)/shard_map/all_to_all | solution.py:610
  27.8 23.0 %all-to-all-start.1 = ((f32[64,1,896]{2,1,0:T(1,128)}), f32[64,1,896]{2,1,0:T(1,128)S(1)}, u32[]{:S(2)}, u32[]{:S(2)}) async-start(f32[64,1,896]{2,1,0:T(1,128)} %bitcast.5), calls=%async_computation.1 | async-start | bytes 458752 | tf_op jit(solution)/shard_map/all_to_all | solution.py:610
  33.1 8.3 %collective-permute-start = (f32[8,256]{1,0:T(8,128)S(1)}, f32[8,256]{1,0:T(8,128)S(1)}, u32[]{:S(2)}, u32[]{:S(2)}) collective-permute-start(f32[8,256]{1,0:T(8,128)S(1)} %get-tuple-element.24), channel_id=1, source_target_pairs={{0,64},{64,128},{128,192},{192,0},{1,65},{65,129},{129,193},{193,1... | collective-permute-start | bytes 24584 | tf_op jit(solution)/shard_map/ppermute | solution.py:606
  36.2 5.3 %collective-permute-start.1 = (f32[8,256]{1,0:T(8,128)S(1)}, f32[8,256]{1,0:T(8,128)S(1)}, u32[]{:S(2)}, u32[]{:S(2)}) collective-permute-start(f32[8,256]{1,0:T(8,128)S(1)} %get-tuple-element.25), channel_id=1, source_target_pairs={{0,192},{64,0},{128,64},{192,128},{1,193},{65,1},{129,65},{193,129... | collective-permute-start | bytes 24584 | tf_op jit(solution)/shard_map/ppermute | solution.py:606
  43.3 10.8 %collective-permute-start.4 = (f32[5,32,128]{2,1,0:T(8,128)S(1)}, f32[5,32,128]{2,1,0:T(8,128)S(1)}, u32[]{:S(2)}, u32[]{:S(2)}) collective-permute-start(f32[5,32,128]{2,1,0:T(8,128)S(1)} %get-tuple-element.35), channel_id=1, source_target_pairs={{0,1},{1,2},{2,3},{3,4},{4,5},{5,6},{6,7},{7,8},{8,9},{9,10},{10,1... | collective-permute-start | bytes 245768 | tf_op jit(solution)/shard_map/ppermute | solution.py:606
  44.8 9.4 %collective-permute-start.5 = (f32[5,32,128]{2,1,0:T(8,128)S(1)}, f32[5,32,128]{2,1,0:T(8,128)S(1)}, u32[]{:S(2)}, u32[]{:S(2)}) collective-permute-start(f32[5,32,128]{2,1,0:T(8,128)S(1)} %get-tuple-element.36), channel_id=1, source_target_pairs={{0,15},{1,0},{2,1},{3,2},{4,3},{5,4},{6,5},{7,6},{8,7},{9,8},{10,9... | collective-permute-start | bytes 245768 | tf_op jit(solution)/shard_map/ppermute | solution.py:606
  48.2 6.0 %collective-permute-start.2 = (f32[8,8,128]{2,1,0:T(8,128)S(1)}, f32[8,8,128]{2,1,0:T(8,128)S(1)}, u32[]{:S(2)}, u32[]{:S(2)}) collective-permute-start(f32[8,8,128]{2,1,0:T(8,128)S(1)} %get-tuple-element.33), channel_id=1, source_target_pairs={{0,16},{16,32},{32,48},{48,0},{1,17},{17,33},{33,49},{49,1},{2,18}... | collective-permute-start | bytes 98312 | tf_op jit(solution)/shard_map/ppermute | solution.py:606
  50.7 3.4 %collective-permute-start.3 = (f32[8,8,128]{2,1,0:T(8,128)S(1)}, f32[8,8,128]{2,1,0:T(8,128)S(1)}, u32[]{:S(2)}, u32[]{:S(2)}) collective-permute-start(f32[8,8,128]{2,1,0:T(8,128)S(1)} %get-tuple-element.34), channel_id=1, source_target_pairs={{0,48},{16,0},{32,16},{48,32},{1,49},{17,1},{33,17},{49,33},{2,50}... | collective-permute-start | bytes 98312 | tf_op jit(solution)/shard_map/ppermute | solution.py:606

commit v2 on v1

--- a/solution.py
+++ b/solution.py
@@ -35,7 +35,8 @@
 ROWS = CZ * CY
 NB, SB, SN = 64, 8, 128
 OWNERS = 64
-NEAR_BLOCKS = 16
+NEAR_BLOCKS = 32
+HEAD = 2
 OUT_ROWS = 10
 BACK_ROWS = 7
 
@@ -52,6 +53,7 @@
 YP, YM = moved(1, 1), moved(1, -1)
 ZP, ZM = moved(2, 1), moved(2, -1)
 MOVING = XP + XM
+PAIRS = list(range(1, 19, 2))
 STILL = moved(0, 0)
 TURNED = [d for d in STILL if lattice_velocity[d][1] != 0]
 BENT = [d for d in MOVING if lattice_velocity[d][1] != 0]
@@ -60,7 +62,7 @@
 
 def signed_sum(values, component):
     total = None
-    for d in range(19):
+    for d in values:
         c = lattice_velocity[d][component]
         if c == 0:
             continue
@@ -73,6 +75,15 @@
     return total
 
 
+def signed_total(v, c):
+    total = None
+    for k in range(3):
+        if c[k] != 0:
+            term = v[k] if c[k] > 0 else -v[k]
+            total = term if total is None else total + term
+    return total
+
+
 def shape(dims, dtype=jnp.float32):
     return jax.ShapeDtypeStruct(dims, dtype)
 
@@ -94,73 +105,117 @@
 
 
 def forces_body(
-    row_hbm, owner_hbm, slot_hbm, pop_hbm, w_hbm, out_ref,
-    row_s, owner_s, slot_s, pop, w, mom, seen, pop_sem, w_sem, in_sem,
+    row_hbm,
+    owner_hbm,
+    slot_hbm,
+    pop_hbm,
+    w_hbm,
+    out_ref,
+    head,
+    place_ref,
+    row_s,
+    owner_v,
+    slot_v,
+    pop,
+    w,
+    mom,
+    made,
+    pop_sem,
+    w_sem,
+    in_sem,
 ):
     parts = 4
     integers = [
         pltpu.make_async_copy(a, b, in_sem.at[i])
-        for i, (a, b) in enumerate(((row_hbm, row_s), (owner_hbm, owner_s), (slot_hbm, slot_s)))
+        for i, (a, b) in enumerate(((owner_hbm, owner_v), (slot_hbm, slot_v), (row_hbm, row_s)))
     ]
     pop_copies = []
     for c in range(parts):
         rows = pl.ds(c * (ROWS // parts), ROWS // parts)
-        pop_copies.append(
-            pltpu.make_async_copy(pop_hbm.at[:, rows], pop.at[:, rows], pop_sem.at[c])
-        )
+        target = head if c == 0 else pop.at[:, pl.ds((c - 1) * (ROWS // parts), ROWS // parts)]
+        pop_copies.append(pltpu.make_async_copy(pop_hbm.at[:, rows], target, pop_sem.at[c]))
     w_copies = []
     for c in range(parts):
         blocks = pl.ds(c * (NB // parts), NB // parts)
         w_copies.append(pltpu.make_async_copy(w_hbm.at[blocks], w.at[blocks], w_sem.at[c]))
-    for copy in pop_copies + integers + w_copies:
+    for copy in integers + pop_copies + w_copies:
         copy.start()
-    out_ref[...] = jnp.zeros(out_ref.shape, jnp.float32)
-    for o in range(OWNERS):
-        seen[o] = 0
+    for copy in integers:
+        copy.wait()
+
+    def iota(dims, axis):
+        return lax.broadcasted_iota(jnp.int32, dims, axis).astype(jnp.float32)
+
+    def number(flags):
+        return jnp.where(flags, 1.0, 0.0)
+
+    square = (NB, NB)
+    owner = owner_v[...].astype(jnp.float32)
+    slot = slot_v[...].astype(jnp.float32)
+    across = jnp.broadcast_to(owner, square)
+    diagonal = iota(square, 0) == iota(square, 1)
+    owner_down = jnp.sum(jnp.where(diagonal, across, 0.0), axis=1, keepdims=True)
+    same = jnp.broadcast_to(owner_down, square) == across
+    rank = jnp.sum(number(same & (iota(square, 0) < iota(square, 1))), axis=0, keepdims=True)
+    rank_down = jnp.sum(
+        number(same & (iota(square, 1) < iota(square, 0))), axis=1, keepdims=True
+    )
+    target = jnp.broadcast_to(owner + OWNERS * rank, (2 * OWNERS, NB))
+    place = number(target == iota((2 * OWNERS, NB), 0))
+    target_down = jnp.broadcast_to(owner_down + OWNERS * rank_down, (NB, 2 * OWNERS))
+    place_ref[...] = number(target_down == iota((NB, 2 * OWNERS), 1))
+    last = jnp.broadcast_to(slot, square) == SB - 1
+    shared = number((across + 1.0 == iota(square, 0)) & last)
+    left = jnp.concatenate([place, shared], axis=0).astype(jnp.bfloat16)
+    tags = jnp.sum(place * (jnp.broadcast_to(slot, (2 * OWNERS, NB)) + 1.0), axis=1, keepdims=True)
+    lane = lax.broadcasted_iota(jnp.int32, (OWNERS, 128), 1)
+    first = jnp.broadcast_to(tags[:OWNERS], (OWNERS, 128))
+    second = jnp.broadcast_to(tags[OWNERS:], (OWNERS, 128))
+    out_ref[pl.ds(9, OWNERS, stride=OUT_ROWS), :] = jnp.where(
+        lane == 0, first, jnp.where(lane == 1, second, 0.0)
+    )
+
     for c in range(parts):
         pop_copies[c].wait()
         for t in range(c * (ROWS // parts // 8), (c + 1) * (ROWS // parts // 8)):
-            values = [pop[d, t * 8 : t * 8 + 8, :] for d in range(19)]
+            ref, at = (head, t * 8) if c == 0 else (pop, t * 8 - ROWS // parts)
+            values = [ref[d, at : at + 8, :] for d in range(19)]
+            gaps = {d: values[d] - values[d + 1] for d in PAIRS}
             for k in range(3):
-                mom[pl.ds(t * 64 + k, 8, stride=8), :] = load_scale * signed_sum(values, k)
-    lane = lax.broadcasted_iota(jnp.int32, (1, 128), 1)
-    for copy in integers:
-        copy.wait()
+                mom[pl.ds(t * 64 + k, 8, stride=8), :] = load_scale * signed_sum(gaps, k)
     for b in range(NB):
         if b % (NB // parts) == 0:
             w_copies[b // (NB // parts)].wait()
         traction = mom[pl.ds(pl.multiple_of(row_s[b] * 8, 8), 8), :].astype(jnp.bfloat16)
-        force = jnp.dot(traction, w[b], preferred_element_type=jnp.float32)[:3]
-        owner = owner_s[b]
-        rank = seen[owner]
-        seen[owner] = rank + 1
-        slot = slot_s[b]
-        start = owner * OUT_ROWS
-        out_ref[pl.ds(start + rank * 3, 3), :] = force
-        pltpu.store(
-            out_ref.at[pl.ds(start + 9, 1), :],
-            jnp.full((1, 128), (slot + 1).astype(jnp.float32)),
-            mask=lane == rank,
-        )
-        shared = jnp.logical_and(slot == SB - 1, owner < OWNERS - 1)
-        after = jnp.where(owner < OWNERS - 1, owner + 1, 0) * OUT_ROWS + 6
-        out_ref[pl.ds(after, 3), :] += jnp.where(shared, force, 0.0)
+        made[b * 8 : b * 8 + 8, :] = jnp.dot(traction, w[b], preferred_element_type=jnp.float32)
+    for k in range(3):
+        high, low = two_parts(made[pl.ds(k, NB, stride=8), :])
+        rows = jnp.dot(left, high, preferred_element_type=jnp.float32)
+        rows = rows + jnp.dot(left, low, preferred_element_type=jnp.float32)
+        for g in range(3):
+            out_ref[pl.ds(3 * g + k, OWNERS, stride=OUT_ROWS), :] = rows[
+                g * OWNERS : (g + 1) * OWNERS
+            ]
 
 
 def send_forces(rows, owners, slots, populations, weights):
     return pl.pallas_call(
         forces_body,
-        out_shape=near((OWNERS * OUT_ROWS, 128)),
+        out_shape=(
+            near((OWNERS * OUT_ROWS, 128)),
+            near((19, HEAD * CY, CX)),
+            near((NB, 2 * OWNERS)),
+        ),
         in_specs=[ANY] * 5,
-        out_specs=VMEM,
+        out_specs=(VMEM, VMEM, VMEM),
         scratch_shapes=[
             pltpu.SMEM((NB,), jnp.int32),
-            pltpu.SMEM((NB,), jnp.int32),
-            pltpu.SMEM((NB,), jnp.int32),
-            pltpu.VMEM((19, ROWS, CX), jnp.float32),
+            pltpu.VMEM((1, NB), jnp.int32),
+            pltpu.VMEM((1, NB), jnp.int32),
+            pltpu.VMEM((19, ROWS - HEAD * CY, CX), jnp.float32),
             pltpu.VMEM((NB, CX, SN), jnp.bfloat16),
             pltpu.VMEM((ROWS * 8, CX), jnp.float32),
-            pltpu.SMEM((OWNERS,), jnp.int32),
+            pltpu.VMEM((NB * 8, SN), jnp.float32),
             pltpu.SemaphoreType.DMA((4,)),
             pltpu.SemaphoreType.DMA((4,)),
             pltpu.SemaphoreType.DMA((3,)),
@@ -176,12 +231,7 @@
     return high, (x - high.astype(jnp.float32)).astype(jnp.bfloat16)
 
 
-def owner_body(in_ref, comp_hbm, near_hbm, yz_ref, disp_ref, back_ref, comp, left, right, sem):
-    copies = [pltpu.make_async_copy(near_hbm, comp.at[SB], sem.at[SB])]
-    for s in range(SB):
-        copies.append(pltpu.make_async_copy(comp_hbm.at[s], comp.at[s], sem.at[s]))
-    for copy in copies:
-        copy.start()
+def owner_body(in_ref, comp_ref, near_ref, yz_ref, disp_ref, back_ref, left, right):
 
     b, e = lax.axis_index("gy"), lax.axis_index("gz")
     for j, d in enumerate(DIAGONAL):
@@ -224,12 +274,10 @@
         first = mm(rows, high)
         return first[:3] + first[3:6] + mm(rows, low)[:3]
 
-    copies[0].wait()
     for s in range(SB):
-        copies[1 + s].wait()
-        moved_by = product(s, comp[s])
+        moved_by = product(s, comp_ref[s])
         if s == 0:
-            moved_by = moved_by + product(SB, comp[SB])
+            moved_by = moved_by + product(SB, near_ref[...])
         disp_ref[:, s, :] = moved_by
         right[s * 8 : s * 8 + 3, :] = moved_by
     chosen = chosen.astype(jnp.bfloat16)
@@ -247,24 +295,20 @@
     return pl.pallas_call(
         owner_body,
         out_shape=(shape((3, SB, SN)), near((OWNERS * BACK_ROWS, 128))),
-        in_specs=[VMEM, ANY, ANY, VMEM],
+        in_specs=[VMEM] * 4,
         out_specs=(VMEM, VMEM),
         scratch_shapes=[
-            pltpu.VMEM((SB + 1, SN, SN), jnp.float32),
             pltpu.VMEM((SB * 8 + 8, 128), jnp.float32),
             pltpu.VMEM((SB * 8, 128), jnp.float32),
-            pltpu.SemaphoreType.DMA((SB + 1,)),
         ],
         cost_estimate=cost(20_000_000, 1_200_000),
         compiler_params=pltpu.CompilerParams(vmem_limit_bytes=16 * 1024 * 1024),
         name="owner",
-    )(held(arrived), far(compliance), far(neighbour), held(lines))
-
-
-def wall_body(owner_hbm, in_ref, w_near, w_hbm, out_ref, owner_s, w, seen, w_sem, in_sem):
-    owner_copy = pltpu.make_async_copy(owner_hbm, owner_s, in_sem)
-    owner_copy.start()
-    parts = 6
+    )(held(arrived), held(compliance), held(neighbour), held(lines))
+
+
+def wall_body(place_ref, in_ref, w_near, w_hbm, out_ref, w, nodes, w_sem):
+    parts = 4
     size = (NB - NEAR_BLOCKS) // parts
     w_copies = []
     for c in range(parts):
@@ -275,9 +319,14 @@
         )
     for copy in w_copies:
         copy.start()
-    for o in range(OWNERS):
-        seen[o] = 0
-    owner_copy.wait()
+    place = place_ref[...].astype(jnp.bfloat16)
+    for k in range(3):
+        arrived = jnp.concatenate(
+            [in_ref[pl.ds(3 * r + k, OWNERS, stride=BACK_ROWS), :] for r in range(2)], axis=0
+        )
+        nodes[pl.ds(k, NB, stride=8), :] = jnp.dot(
+            place, arrived.astype(jnp.bfloat16), preferred_element_type=jnp.float32
+        )
     for b in range(NB):
         if b < NEAR_BLOCKS:
             weight = w_near[b]
@@ -285,36 +334,35 @@
             if (b - NEAR_BLOCKS) % size == 0:
                 w_copies[(b - NEAR_BLOCKS) // size].wait()
             weight = w[b - NEAR_BLOCKS]
-        owner = owner_s[b]
-        rank = seen[owner]
-        seen[owner] = rank + 1
-        nodes = in_ref[pl.ds(owner * BACK_ROWS + rank * 3, 3), :].astype(jnp.bfloat16)
-        out_ref[:, b, :] = lax.dot_general(
-            nodes, weight, (((1,), (1,)), ((), ())), preferred_element_type=jnp.float32
+        motion = lax.dot_general(
+            nodes[b * 8 : b * 8 + 8, :].astype(jnp.bfloat16),
+            weight,
+            (((1,), (1,)), ((), ())),
+            preferred_element_type=jnp.float32,
         )
-
-
-def wall_step(owners, arrived, first_weights, weights):
+        out_ref[:, b, :] = motion[:3]
+
+
+def wall_step(place, arrived, first_weights, weights):
     return pl.pallas_call(
         wall_body,
         out_shape=shape((3, NB, CX)),
-        in_specs=[ANY, VMEM, VMEM, ANY],
+        in_specs=[VMEM, VMEM, VMEM, ANY],
         out_specs=VMEM,
         scratch_shapes=[
-            pltpu.SMEM((NB,), jnp.int32),
             pltpu.VMEM((NB - NEAR_BLOCKS, CX, SN), jnp.bfloat16),
-            pltpu.SMEM((OWNERS,), jnp.int32),
-            pltpu.SemaphoreType.DMA((6,)),
-            pltpu.SemaphoreType.DMA,
+            pltpu.VMEM((NB * 8, SN), jnp.float32),
+            pltpu.SemaphoreType.DMA((4,)),
         ],
         cost_estimate=cost(20_000_000, 2_500_000),
         compiler_params=pltpu.CompilerParams(vmem_limit_bytes=16 * 1024 * 1024),
         name="wall",
-    )(far(owners), held(arrived), held(first_weights), far(weights))
+    )(held(place), held(arrived), held(first_weights), far(weights))
 
 
 def collide_body(
     pop_hbm,
+    head,
     new_hbm,
     rel_ref,
     xp_ref,
@@ -333,36 +381,45 @@
     pop_sem,
 ):
     arriving = [
-        pltpu.make_async_copy(pop_hbm.at[:, z], pop.at[:, z], pop_sem.at[z]) for z in range(CZ)
+        pltpu.make_async_copy(pop_hbm.at[:, z], pop.at[:, z - HEAD], pop_sem.at[z])
+        for z in range(HEAD, CZ)
     ]
     for copy in arriving:
         copy.start()
     lane = lax.broadcasted_iota(jnp.int32, (8, 128), 1)
     for z in range(CZ):
-        arriving[z].wait()
+        if z >= HEAD:
+            arriving[z - HEAD].wait()
         for t in range(CY // 8):
             rows = pl.ds(t * 8, 8)
-            f = [pop[d, z, rows, :] for d in range(19)]
+            if z < HEAD:
+                f = [head[d, z * CY + t * 8 : z * CY + t * 8 + 8, :] for d in range(19)]
+            else:
+                f = [pop[d, z - HEAD, rows, :] for d in range(19)]
+            sums = {d: f[d] + f[d + 1] for d in PAIRS}
+            gaps = {d: f[d] - f[d + 1] for d in PAIRS}
             density = f[0]
-            for d in range(1, 19):
-                density = density + f[d]
+            for d in PAIRS:
+                density = density + sums[d]
             inverse = 1.0 / density
-            v = [signed_sum(f, k) * inverse for k in range(3)]
+            v = [signed_sum(gaps, k) * inverse for k in range(3)]
             speed_square = v[0] * v[0] + v[1] * v[1] + v[2] * v[2]
             base = 1.0 - 1.5 * speed_square
-            weighted = {w: (relaxation * w) * density for w in set(lattice_weight)}
+            share = {w: (relaxation * w) * density for w in set(lattice_weight)}
+            steady = {w: share[w] * base for w in set(lattice_weight)}
+            slope = {w: (3.0 * relaxation * w) * density for w in set(lattice_weight)}
+            values = {0: (1.0 - relaxation) * f[0] + steady[lattice_weight[0]]}
+            for d in PAIRS:
+                w = lattice_weight[d]
+                projected = signed_total(v, lattice_velocity[d])
+                odd = slope[w] * projected
+                even = steady[w] + 1.5 * (odd * projected)
+                values[d] = (1.0 - relaxation) * f[d] + (even + odd)
+                values[d + 1] = (1.0 - relaxation) * f[d + 1] + (even - odd)
             pack = jnp.zeros((8, 128), jnp.float32)
             for d in range(19):
                 c = lattice_velocity[d]
-                projected = None
-                for k in range(3):
-                    if c[k] != 0:
-                        term = v[k] if c[k] > 0 else -v[k]
-                        projected = term if projected is None else projected + term
-                bracket = base
-                if projected is not None:
-                    bracket = bracket + projected * (3.0 + 4.5 * projected)
-                value = (1.0 - relaxation) * f[d] + weighted[lattice_weight[d]] * bracket
+                value = values[d]
                 if c[0] > 0:
                     i = XP.index(d)
                     value = pltpu.roll(value, 1, 1)
@@ -431,7 +488,7 @@
             zm_ref[ZM.index(d)] = value
 
 
-def collide_step(populations):
+def collide_step(populations, head):
     return pl.pallas_call(
         collide_body,
         out_shape=(
@@ -446,10 +503,10 @@
             near((6, CZ, 8, CX)),
             near((8, CX)),
         ),
-        in_specs=[ANY],
+        in_specs=[ANY, VMEM],
         out_specs=(ANY,) + (VMEM,) * 9,
         scratch_shapes=[
-            pltpu.VMEM((19, CZ, CY, CX), jnp.float32),
+            pltpu.VMEM((19, CZ - HEAD, CY, CX), jnp.float32),
             pltpu.VMEM((ROWS, 128), jnp.float32),
             pltpu.VMEM((9, CZ, CY, CX), jnp.float32),
             pltpu.VMEM((9, CZ, CY, CX), jnp.float32),
@@ -459,7 +516,7 @@
         cost_estimate=cost(10_000_000, 5_000_000),
         compiler_params=pltpu.CompilerParams(vmem_limit_bytes=16 * 1024 * 1024),
         name="collide",
-    )(far(populations))
+    )(far(populations), held(head))
 
 
 def stream_body(
@@ -613,13 +670,13 @@
 def body(
     populations, rbf_weights, owner_map, shell_slot, compliance, neighbour_compliance, interface_row
 ):
-    owners = owner_map.reshape(NB)
-    slots = shell_slot.reshape(NB)
-    outgoing = send_forces(
+    owners = owner_map.reshape(1, NB)
+    slots = shell_slot.reshape(1, NB)
+    outgoing, head, place = send_forces(
         interface_row, owners, slots, populations.reshape(19, ROWS, CX), rbf_weights
     )
     incoming = exchange(outgoing.reshape(OWNERS, 1, OUT_ROWS * 128))
-    new, relaxed, xp, xm, yp, ym, zp, zm, still, lines = collide_step(populations)
+    new, relaxed, xp, xm, yp, ym, zp, zm, still, lines = collide_step(populations, head)
     xlo = from_behind(xp, "gx", 1)
     xhi = from_behind(xm, "gx", -1)
     displacement, back = owner_step(
@@ -634,7 +691,7 @@
     zlo = from_behind(zp, "gz", 1)
     zhi = from_behind(zm, "gz", -1)
     arrived = arrived.reshape(OWNERS * BACK_ROWS, 128)
-    wall_motion = wall_step(owners, arrived, weights, rbf_weights)
+    wall_motion = wall_step(place, arrived, weights, rbf_weights)
     new = finish_step(new, still, bent, ylo, yhi, zlo, zhi, arrived)
     return (new, displacement.transpose(1, 0, 2), wall_motion.transpose(1, 0, 2))
 

time: 55.5 us -> 54.6 us (0.984)
  Pallas kernels: 17.3 us -> 15.2 us
  waiting for transfers between devices: 8.67 us -> 9.83 us
    pallas_call x1, Pallas kernels: 2.98 us -> 1.42 us  [owner_step(): pl.pallas_call(owner_body, out_shape=(shape((3, SB, SN)), near((OWNERS *...]
    ppermute x6, waiting for transfers between devices: 3.04 us -> 3.85 us  [from_behind(): return lax.ppermute(value, axis, pairs)]
  transfers between devices with their start and end apart: 8 -> 8, of which waited for: 2 -> 3; matrix products, arithmetic and copies ran while one was open for 0% -> 0% of each run, Pallas kernels for 17% -> 16%
where the time goes in v2:
time: 54.6 us; the launch traced here: 54.3 us
  starting transfers between devices  28.5 us (52%)
  Pallas kernels  15.2 us (28%)
  waiting for transfers between devices  9.83 us (18%)
  between operations  0.71 us (1%)
    all_to_all x2, starting transfers between devices, exchange(): lax.all_to_all(value, ('gy', 'gz'), split_axis=0, concat_axis=0, tiled=True)  15.8 us
    ppermute x6, starting transfers between devices, from_behind(): return lax.ppermute(value, axis, pairs)  12.7 us
    all_to_all x2, waiting for transfers between devices, exchange(): lax.all_to_all(value, ('gy', 'gz'), split_axis=0, concat_axis=0, tiled=True)  5.98 us
    pallas_call x1, Pallas kernels, send_forces(): pl.pallas_call(forces_body, out_shape=(near((OWNERS * OUT_ROWS, 128)), ne...  4.23 us
    ppermute x6, waiting for transfers between devices, from_behind(): return lax.ppermute(value, axis, pairs)  3.85 us
    pallas_call x1, Pallas kernels, collide_step(): pl.pallas_call(collide_body, out_shape=(shape((19, CZ, CY, CX)), near((10...  3.74 us
    pallas_call x1, Pallas kernels, wall_step(): pl.pallas_call(wall_body, out_shape=shape((3, NB, CX)), in_specs=[VMEM, V...  2.72 us
    pallas_call x1, Pallas kernels, stream_step(): pl.pallas_call(stream_body, out_shape=(shape((19, CZ, CY, CX)), near((CZ,...  2.14 us
  transfers between devices with their start and end apart: 8, of which 3 were waited for; matrix products, arithmetic and copies ran while one was open for 0% of the time, Pallas kernels for 16%

profile of v2, /device:TPU:1, one launch (start us, length us, event | category | flops | bytes accessed | tf_op | source)
XLA Modules:
  0.0 54.3 jit_solution(10444257159727189963)
XLA Ops:
  0.6 4.2 %forces.1 = (f32[640,128]{1,0:T(8,128)}, f32[19,64,128]{2,1,0:T(8,128)S(1)}, f32[64,128]{1,0:T(8,128)S(1)}) custom-call(s32[64]{0:T(128)} %row_hbm.1, s32[1,64]{1,0:T(1,128)} %bitcast.14, s32[1,64]{1,0:T(1,128)} %bitcast.15, f32[19,256,128]{2,1,0:T(8,128)} %bitcast.12, bf16[64,128,128]{2,1,0:T(8,128)(2,1)} %w_hbm.5), custom_call_target="tpu_custom_call" | custom-call | flops 50000000 | bytes 5000000 | tf_op jit(solution)/shard_map/forces/pallas_call | solution.py:202
  4.9 0.0 copy-start
  4.9 0.0 copy-start.1
  4.9 10.5 %all-to-all-start = ((f32[64,1,1280]{2,1,0:T(1,128)}), f32[64,1,1280]{2,1,0:T(1,128)S(1)}, u32[]{:S(2)}, u32[]{:S(2)}) async-start(f32[64,1,1280]{2,1,0:T(1,128)} %bitcast.3), calls=%async_computation | async-start | bytes 655360 | tf_op jit(solution)/shard_map/all_to_all | solution.py:667
  15.4 3.7 %collide.1 = (f32[19,8,32,128]{3,2,1,0:T(8,128)}, f32[10,8,32,128]{3,2,1,0:T(8,128)S(1)}, f32[8,256]{1,0:T(8,128)S(1)}, f32[8,256]{1,0:T(8,128)S(1)}, f32[8,8,12...) custom-call(f32[19,8,32,128]{3,2,1,0:T(8,128)} %pop_hbm.1, ...), custom_call_target="tpu_custom_call" | custom-call | flops 10000000 | bytes 5000000 | tf_op jit(solution)/shard_map/collide/pallas_call | solution.py:492
  19.1 6.0 %all-to-all-done = f32[64,1,1280]{2,1,0:T(1,128)S(1)} async-done(((f32[64,1,1280]{2,1,0:T(1,128)}), f32[64,1,1280]{2,1,0:T(1,128)S(1)}, u32[]{:S(2)}, u32[]{:S(2)}) %all-to-all-start) | async-done | bytes 327712 | tf_op jit(solution)/shard_map/all_to_all | solution.py:667
  25.1 0.0 copy-done
  25.1 0.0 copy-done.1
  25.1 1.4 %owner.1 = (f32[3,8,128]{2,1,0:T(8,128)}, f32[448,128]{1,0:T(8,128)}) custom-call(f32[640,128]{1,0:T(8,128)S(1)} %bitcast.11, f32[8,128,128]{2,1,0:T(8,128)S(1)} %copy-done, f32[128,128]{1,0:T(8,128)S(1)} %copy-done.1, f32[8,128]{1,0:T(8,128)S(1)} %get-tuple-element.42.yz_ref), custom_call_target="tpu_custom_call" | custom-call | flops 20000000 | bytes 1200000 | tf_op jit(solution)/shard_map/owner/pallas_call | solution.py:295
  26.5 5.4 %all-to-all-start.1 = ((f32[64,1,896]{2,1,0:T(1,128)}), f32[64,1,896]{2,1,0:T(1,128)S(1)}, u32[]{:S(2)}, u32[]{:S(2)}) async-start(f32[64,1,896]{2,1,0:T(1,128)} %bitcast.5), calls=%async_computation.1 | async-start | bytes 458752 | tf_op jit(solution)/shard_map/all_to_all | solution.py:667
  31.9 3.1 %collective-permute-start = (f32[8,256]{1,0:T(8,128)S(1)}, f32[8,256]{1,0:T(8,128)S(1)}, u32[]{:S(2)}, u32[]{:S(2)}) collective-permute-start(f32[8,256]{1,0:T(8,128)S(1)} %get-tuple-element.28), channel_id=1, source_target_pairs={{0,64},{64,128},{128,192},{192,0},{1,65},{65,129},{129,193},{193,1... | collective-permute-start | bytes 24584 | tf_op jit(solution)/shard_map/ppermute | solution.py:663
  35.0 2.2 %collective-permute-start.1 = (f32[8,256]{1,0:T(8,128)S(1)}, f32[8,256]{1,0:T(8,128)S(1)}, u32[]{:S(2)}, u32[]{:S(2)}) collective-permute-start(f32[8,256]{1,0:T(8,128)S(1)} %get-tuple-element.29), channel_id=1, source_target_pairs={{0,192},{64,0},{128,64},{192,128},{1,193},{65,1},{129,65},{193,129... | collective-permute-start | bytes 24584 | tf_op jit(solution)/shard_map/ppermute | solution.py:663
  37.2 3.0 %collective-permute-done.lo_ref = f32[8,256]{1,0:T(8,128)S(1)} collective-permute-done((f32[8,256]{1,0:T(8,128)S(1)}, f32[8,256]{1,0:T(8,128)S(1)}, u32[]{:S(2)}, u32[]{:S(2)}) %collective-permute-start) | collective-permute-done | bytes 8224 | tf_op jit(solution)/shard_map/ppermute | solution.py:663
  40.2 0.0 collective-permute-done.1.hi_ref
  40.2 2.1 %stream.1 = (f32[19,8,32,128]{3,2,1,0:T(8,128)}, f32[8,8,128]{2,1,0:T(8,128)}, f32[8,8,128]{2,1,0:T(8,128)}, f32[5,32,128]{2,1,0:T(8,128)S(1)}, f32[5,32,128]{2,...) custom-call(f32[19,8,32,128]{3,2,1,0:T(8,128)} %get-tuple-element.26, ...), custom_call_target="tpu_custom_call", output_to_operand_aliasing={{0}: (0, {})} | custom-call | flops 10000000 | bytes 5000000 | tf_op jit(solution)/shard_map/stream/pallas_call | solution.py:578
  42.4 1.5 %collective-permute-start.4 = (f32[5,32,128]{2,1,0:T(8,128)S(1)}, f32[5,32,128]{2,1,0:T(8,128)S(1)}, u32[]{:S(2)}, u32[]{:S(2)}) collective-permute-start(f32[5,32,128]{2,1,0:T(8,128)S(1)} %get-tuple-element.39), channel_id=1, source_target_pairs={{0,1},{1,2},{2,3},{3,4},{4,5},{5,6},{6,7},{7,8},{8,9},{9,10},{10,1... | collective-permute-start | bytes 245768 | tf_op jit(solution)/shard_map/ppermute | solution.py:663
  43.9 3.4 %collective-permute-start.5 = (f32[5,32,128]{2,1,0:T(8,128)S(1)}, f32[5,32,128]{2,1,0:T(8,128)S(1)}, u32[]{:S(2)}, u32[]{:S(2)}) collective-permute-start(f32[5,32,128]{2,1,0:T(8,128)S(1)} %get-tuple-element.40), channel_id=1, source_target_pairs={{0,15},{1,0},{2,1},{3,2},{4,3},{5,4},{6,5},{7,6},{8,7},{9,8},{10,9... | collective-permute-start | bytes 245768 | tf_op jit(solution)/shard_map/ppermute | solution.py:663
  47.2 2.5 %collective-permute-start.2 = (f32[8,8,128]{2,1,0:T(8,128)}, f32[8,8,128]{2,1,0:T(8,128)S(1)}, u32[]{:S(2)}, u32[]{:S(2)}) collective-permute-start(f32[8,8,128]{2,1,0:T(8,128)} %get-tuple-element.37), channel_id=1, source_target_pairs={{0,16},{16,32},{32,48},{48,0},{1,17},{17,33},{33,49},{49,1},{2,18}... | collective-permute-start | bytes 98312 | tf_op jit(solution)/shard_map/ppermute | solution.py:663
  49.8 0.0 collective-permute-start.3
  49.8 0.0 all-to-all-done.1
  49.8 2.7 %wall.1 = f32[3,64,128]{2,1,0:T(8,128)} custom-call(f32[64,128]{1,0:T(8,128)S(1)} %get-tuple-element.45.place_ref, f32[448,128]{1,0:T(8,128)S(1)} %bitcast.9, bf16[32,128,128]{2,1,0:T(8,128)(2,1)S(1)} %get-tuple-element.46.w_near, bf16[64,128,128]{2,1,0:T(8,128)(2,1)} %w_hbm.5), custom_call_target="tpu_custom_call" | custom-call | flops 20000000 | bytes 2500000 | tf_op jit(solution)/shard_map/wall/pallas_call | solution.py:347
  52.5 0.0 collective-permute-done.2.ylo
  52.5 0.8 %collective-permute-done.3.yhi = f32[8,8,128]{2,1,0:T(8,128)S(1)} collective-permute-done((f32[8,8,128]{2,1,0:T(8,128)}, f32[8,8,128]{2,1,0:T(8,128)S(1)}, u32[]{:S(2)}, u32[]{:S(2)}) %collective-permute-start.3) | collective-permute-done | bytes 32800 | tf_op jit(solution)/shard_map/ppermute | solution.py:663
  53.3 0.0 collective-permute-done.4.zlo
  53.3 0.0 collective-permute-done.5.zhi
  53.3 0.9 %finish.1 = f32[19,8,32,128]{3,2,1,0:T(8,128)} custom-call(f32[19,8,32,128]{3,2,1,0:T(8,128)} %get-tuple-element.34.new_in, f32[6,8,8,128]{3,2,1,0:T(8,128)S(1)} %get-tuple-element.35.still_ref, f32[4,8,8,128]{3,2,1,0:T(8,128)S(1)} %get-tuple-element.36.moving_ref, f32[8,8,128]{2,1,0:T(8,128)S(1)} %collective-permute-done.2.ylo, ...), custom_call_target="tpu_custom_call", output_to_operand_aliasing={{}: (0, {})} | custom-call | flops 100000 | bytes 1000000 | tf_op jit(solution)/shard_map/finish/pallas_call | solution.py:643
Async XLA Ops:
  4.9 20.2 %copy-start = (f32[8,128,128]{2,1,0:T(8,128)S(1)}, f32[8,128,128]{2,1,0:T(8,128)}, u32[]{:S(2)}) copy-start(f32[8,128,128]{2,1,0:T(8,128)} %comp_ref.1) | copy-start | bytes 1572868
  4.9 20.2 %copy-start.1 = (f32[128,128]{1,0:T(8,128)S(1)}, f32[128,128]{1,0:T(8,128)}, u32[]{:S(2)}) copy-start(f32[128,128]{1,0:T(8,128)} %near_ref.1) | copy-start | bytes 196612
  4.9 20.2 %all-to-all-start = ((f32[64,1,1280]{2,1,0:T(1,128)}), f32[64,1,1280]{2,1,0:T(1,128)S(1)}, u32[]{:S(2)}, u32[]{:S(2)}) async-start(f32[64,1,1280]{2,1,0:T(1,128)} %bitcast.3), calls=%async_computation | async-start | bytes 655360 | tf_op jit(solution)/shard_map/all_to_all | solution.py:667
  26.5 23.2 %all-to-all-start.1 = ((f32[64,1,896]{2,1,0:T(1,128)}), f32[64,1,896]{2,1,0:T(1,128)S(1)}, u32[]{:S(2)}, u32[]{:S(2)}) async-start(f32[64,1,896]{2,1,0:T(1,128)} %bitcast.5), calls=%async_computation.1 | async-start | bytes 458752 | tf_op jit(solution)/shard_map/all_to_all | solution.py:667
  31.9 8.3 %collective-permute-start = (f32[8,256]{1,0:T(8,128)S(1)}, f32[8,256]{1,0:T(8,128)S(1)}, u32[]{:S(2)}, u32[]{:S(2)}) collective-permute-start(f32[8,256]{1,0:T(8,128)S(1)} %get-tuple-element.28), channel_id=1, source_target_pairs={{0,64},{64,128},{128,192},{192,0},{1,65},{65,129},{129,193},{193,1... | collective-permute-start | bytes 24584 | tf_op jit(solution)/shard_map/ppermute | solution.py:663
  35.0 5.3 %collective-permute-start.1 = (f32[8,256]{1,0:T(8,128)S(1)}, f32[8,256]{1,0:T(8,128)S(1)}, u32[]{:S(2)}, u32[]{:S(2)}) collective-permute-start(f32[8,256]{1,0:T(8,128)S(1)} %get-tuple-element.29), channel_id=1, source_target_pairs={{0,192},{64,0},{128,64},{192,128},{1,193},{65,1},{129,65},{193,129... | collective-permute-start | bytes 24584 | tf_op jit(solution)/shard_map/ppermute | solution.py:663
  42.4 11.0 %collective-permute-start.4 = (f32[5,32,128]{2,1,0:T(8,128)S(1)}, f32[5,32,128]{2,1,0:T(8,128)S(1)}, u32[]{:S(2)}, u32[]{:S(2)}) collective-permute-start(f32[5,32,128]{2,1,0:T(8,128)S(1)} %get-tuple-element.39), channel_id=1, source_target_pairs={{0,1},{1,2},{2,3},{3,4},{4,5},{5,6},{6,7},{7,8},{8,9},{9,10},{10,1... | collective-permute-start | bytes 245768 | tf_op jit(solution)/shard_map/ppermute | solution.py:663
  43.9 9.5 %collective-permute-start.5 = (f32[5,32,128]{2,1,0:T(8,128)S(1)}, f32[5,32,128]{2,1,0:T(8,128)S(1)}, u32[]{:S(2)}, u32[]{:S(2)}) collective-permute-start(f32[5,32,128]{2,1,0:T(8,128)S(1)} %get-tuple-element.40), channel_id=1, source_target_pairs={{0,15},{1,0},{2,1},{3,2},{4,3},{5,4},{6,5},{7,6},{8,7},{9,8},{10,9... | collective-permute-start | bytes 245768 | tf_op jit(solution)/shard_map/ppermute | solution.py:663
  47.2 5.3 %collective-permute-start.2 = (f32[8,8,128]{2,1,0:T(8,128)}, f32[8,8,128]{2,1,0:T(8,128)S(1)}, u32[]{:S(2)}, u32[]{:S(2)}) collective-permute-start(f32[8,8,128]{2,1,0:T(8,128)} %get-tuple-element.37), channel_id=1, source_target_pairs={{0,16},{16,32},{32,48},{48,0},{1,17},{17,33},{33,49},{49,1},{2,18}... | collective-permute-start | bytes 98312 | tf_op jit(solution)/shard_map/ppermute | solution.py:663
  49.8 3.6 %collective-permute-start.3 = (f32[8,8,128]{2,1,0:T(8,128)}, f32[8,8,128]{2,1,0:T(8,128)S(1)}, u32[]{:S(2)}, u32[]{:S(2)}) collective-permute-start(f32[8,8,128]{2,1,0:T(8,128)} %get-tuple-element.38), channel_id=1, source_target_pairs={{0,48},{16,0},{32,16},{48,32},{1,49},{17,1},{33,17},{49,33},{2,50}... | collective-permute-start | bytes 98312 | tf_op jit(solution)/shard_map/ppermute | solution.py:663

commit v3 on v2

--- a/solution.py
+++ b/solution.py
@@ -35,7 +35,6 @@
 ROWS = CZ * CY
 NB, SB, SN = 64, 8, 128
 OWNERS = 64
-NEAR_BLOCKS = 32
 HEAD = 2
 OUT_ROWS = 10
 BACK_ROWS = 7
@@ -135,8 +134,9 @@
         target = head if c == 0 else pop.at[:, pl.ds((c - 1) * (ROWS // parts), ROWS // parts)]
         pop_copies.append(pltpu.make_async_copy(pop_hbm.at[:, rows], target, pop_sem.at[c]))
     w_copies = []
-    for c in range(parts):
-        blocks = pl.ds(c * (NB // parts), NB // parts)
+    pieces = 8
+    for c in range(pieces):
+        blocks = pl.ds(c * (NB // pieces), NB // pieces)
         w_copies.append(pltpu.make_async_copy(w_hbm.at[blocks], w.at[blocks], w_sem.at[c]))
     for copy in integers + pop_copies + w_copies:
         copy.start()
@@ -184,8 +184,8 @@
             for k in range(3):
                 mom[pl.ds(t * 64 + k, 8, stride=8), :] = load_scale * signed_sum(gaps, k)
     for b in range(NB):
-        if b % (NB // parts) == 0:
-            w_copies[b // (NB // parts)].wait()
+        if b % (NB // pieces) == 0:
+            w_copies[b // (NB // pieces)].wait()
         traction = mom[pl.ds(pl.multiple_of(row_s[b] * 8, 8), 8), :].astype(jnp.bfloat16)
         made[b * 8 : b * 8 + 8, :] = jnp.dot(traction, w[b], preferred_element_type=jnp.float32)
     for k in range(3):
@@ -217,7 +217,7 @@
             pltpu.VMEM((ROWS * 8, CX), jnp.float32),
             pltpu.VMEM((NB * 8, SN), jnp.float32),
             pltpu.SemaphoreType.DMA((4,)),
-            pltpu.SemaphoreType.DMA((4,)),
+            pltpu.SemaphoreType.DMA((8,)),
             pltpu.SemaphoreType.DMA((3,)),
         ],
         cost_estimate=cost(50_000_000, 5_000_000),
@@ -305,59 +305,6 @@
         compiler_params=pltpu.CompilerParams(vmem_limit_bytes=16 * 1024 * 1024),
         name="owner",
     )(held(arrived), held(compliance), held(neighbour), held(lines))
-
-
-def wall_body(place_ref, in_ref, w_near, w_hbm, out_ref, w, nodes, w_sem):
-    parts = 4
-    size = (NB - NEAR_BLOCKS) // parts
-    w_copies = []
-    for c in range(parts):
-        w_copies.append(
-            pltpu.make_async_copy(
-                w_hbm.at[pl.ds(NEAR_BLOCKS + c * size, size)], w.at[pl.ds(c * size, size)], w_sem.at[c]
-            )
-        )
-    for copy in w_copies:
-        copy.start()
-    place = place_ref[...].astype(jnp.bfloat16)
-    for k in range(3):
-        arrived = jnp.concatenate(
-            [in_ref[pl.ds(3 * r + k, OWNERS, stride=BACK_ROWS), :] for r in range(2)], axis=0
-        )
-        nodes[pl.ds(k, NB, stride=8), :] = jnp.dot(
-            place, arrived.astype(jnp.bfloat16), preferred_element_type=jnp.float32
-        )
-    for b in range(NB):
-        if b < NEAR_BLOCKS:
-            weight = w_near[b]
-        else:
-            if (b - NEAR_BLOCKS) % size == 0:
-                w_copies[(b - NEAR_BLOCKS) // size].wait()
-            weight = w[b - NEAR_BLOCKS]
-        motion = lax.dot_general(
-            nodes[b * 8 : b * 8 + 8, :].astype(jnp.bfloat16),
-            weight,
-            (((1,), (1,)), ((), ())),
-            preferred_element_type=jnp.float32,
-        )
-        out_ref[:, b, :] = motion[:3]
-
-
-def wall_step(place, arrived, first_weights, weights):
-    return pl.pallas_call(
-        wall_body,
-        out_shape=shape((3, NB, CX)),
-        in_specs=[VMEM, VMEM, VMEM, ANY],
-        out_specs=VMEM,
-        scratch_shapes=[
-            pltpu.VMEM((NB - NEAR_BLOCKS, CX, SN), jnp.bfloat16),
-            pltpu.VMEM((NB * 8, SN), jnp.float32),
-            pltpu.SemaphoreType.DMA((4,)),
-        ],
-        cost_estimate=cost(20_000_000, 2_500_000),
-        compiler_params=pltpu.CompilerParams(vmem_limit_bytes=16 * 1024 * 1024),
-        name="wall",
-    )(held(place), held(arrived), held(first_weights), far(weights))
 
 
 def collide_body(
@@ -447,10 +394,8 @@
         if cy == 0:
             source = still.at[i, pl.ds(first - cz, count)]
         else:
-            spread(
-                d, lambda z: still[i, z], turned_to.at[i], edge_ref.at[TURNED.index(d)],
-                yp_ref, ym_ref, zp_ref, zm_ref,
-            )
+            faces = (yp_ref, ym_ref, zp_ref, zm_ref)
+            spread(d, lambda z: still[i, z], turned_to.at[i], edge_ref.at[TURNED.index(d)], faces)
             source = turned_to.at[i, pl.ds(first, count)]
         if d in DIAGONAL:
             at = CZ - 1 if cz > 0 else 0
@@ -466,15 +411,19 @@
         copy.wait()
 
 
-def spread(d, plane_of, res, edge, yp_ref, ym_ref, zp_ref, zm_ref):
+def spread(d, plane_of, res, edge, faces):
     _, cy, cz = lattice_velocity[d]
     for z in range(CZ):
+        if faces is None and not 0 <= z + cz < CZ:
+            continue
         value = plane_of(z)
         if cy > 0:
-            yp_ref[z, YP.index(d) : YP.index(d) + 1, :] = value[CY - 1 : CY]
+            if faces is not None:
+                faces[0][z, YP.index(d) : YP.index(d) + 1, :] = value[CY - 1 : CY]
             value = pltpu.roll(value, 1, 0)
         elif cy < 0:
-            ym_ref[z, YM.index(d) : YM.index(d) + 1, :] = value[0:1]
+            if faces is not None:
+                faces[1][z, YM.index(d) : YM.index(d) + 1, :] = value[0:1]
             value = pltpu.roll(value, CY - 1, 0)
         if 0 <= z + cz < CZ:
             res[z + cz] = value
@@ -483,9 +432,9 @@
             elif cy < 0:
                 edge[z + cz] = value[CY - 8 :]
         elif cz > 0:
-            zp_ref[ZP.index(d)] = value
+            faces[2][ZP.index(d)] = value
         else:
-            zm_ref[ZM.index(d)] = value
+            faces[3][ZM.index(d)] = value
 
 
 def collide_step(populations, head):
@@ -519,30 +468,18 @@
     )(far(populations), held(head))
 
 
-def stream_body(
-    new_in,
-    w_hbm,
-    rel,
-    lo_ref,
-    hi_ref,
-    yp_in,
-    ym_in,
-    zp_in,
-    zm_in,
-    new_hbm,
-    yp_ref,
-    ym_ref,
-    zp_ref,
-    zm_ref,
-    edge_ref,
-    w_ref,
-    res,
-    cols,
-    sem,
-    w_sem,
+def patched(rel, cols, j, z, first, count):
+    cx = lattice_velocity[MOVING[j]][0]
+    side, i, at = (0, j, 0) if cx > 0 else (1, j - 5, CX - 1)
+    lane = lax.broadcasted_iota(jnp.int32, (count, CX), 1)
+    start = z * CY + first
+    column = jnp.broadcast_to(cols[side, start : start + count, i : i + 1], (count, CX))
+    return jnp.where(lane == at, column, rel[j, z, first : first + count, :])
+
+
+def faces_body(
+    rel, lo_ref, hi_ref, yp_in, ym_in, zp_in, zm_in, yp_ref, ym_ref, zp_ref, zm_ref, cols
 ):
-    w_copy = pltpu.make_async_copy(w_hbm.at[pl.ds(0, NEAR_BLOCKS)], w_ref, w_sem)
-    w_copy.start()
     yp_ref[...] = yp_in[...]
     ym_ref[...] = ym_in[...]
     zp_ref[...] = zp_in[...]
@@ -552,53 +489,112 @@
         for side, ref in enumerate((lo_ref, hi_ref)):
             block = jnp.concatenate([ref[:, h * 128 : h * 128 + 128], pad], axis=0)
             cols[side, h * 128 : h * 128 + 128, :] = block.T
-    lane = lax.broadcasted_iota(jnp.int32, (CY, CX), 1)
+    for j, d in enumerate(MOVING):
+        _, cy, cz = lattice_velocity[d]
+        if cz > 0:
+            zp_ref[ZP.index(d)] = patched(rel, cols, j, CZ - 1, 0, CY)
+        elif cz < 0:
+            zm_ref[ZM.index(d)] = patched(rel, cols, j, 0, 0, CY)
+        for z in range(CZ):
+            if cy > 0:
+                i = YP.index(d)
+                yp_ref[z, i : i + 1, :] = patched(rel, cols, j, z, CY - 8, 8)[7:8]
+            elif cy < 0:
+                i = YM.index(d)
+                ym_ref[z, i : i + 1, :] = patched(rel, cols, j, z, 0, 8)[0:1]
+
+
+def faces_step(moving, below, above, faces):
+    return pl.pallas_call(
+        faces_body,
+        out_shape=(
+            near((CZ, 8, CX)),
+            near((CZ, 8, CX)),
+            near((5, CY, CX)),
+            near((5, CY, CX)),
+            near((2, ROWS, 128)),
+        ),
+        in_specs=[VMEM] * 7,
+        out_specs=(VMEM,) * 5,
+        cost_estimate=cost(1_000_000, 500_000),
+        compiler_params=pltpu.CompilerParams(vmem_limit_bytes=16 * 1024 * 1024),
+        name="faces",
+    )(held(moving), held(below), held(above), *[held(f) for f in faces])
+
+
+def bulk_body(
+    new_in,
+    w_hbm,
+    rel,
+    cols,
+    place_ref,
+    in_ref,
+    new_hbm,
+    edge_ref,
+    out_ref,
+    w,
+    nodes,
+    res,
+    sem,
+    w_sem,
+):
+    parts = 8
+    w_copies = []
+    for c in range(parts):
+        blocks = pl.ds(c * (NB // parts), NB // parts)
+        w_copies.append(pltpu.make_async_copy(w_hbm.at[blocks], w.at[blocks], w_sem.at[c]))
+    for copy in w_copies:
+        copy.start()
     copies = []
     for j, d in enumerate(MOVING):
-        cx, cy, cz = lattice_velocity[d]
-        side, i, at = (0, j, 0) if cx > 0 else (1, j - 5, CX - 1)
-
-        def plane(z):
-            column = jnp.broadcast_to(cols[side, z * CY : (z + 1) * CY, i : i + 1], (CY, CX))
-            return jnp.where(lane == at, column, rel[j, z])
-
+        _, cy, cz = lattice_velocity[d]
         edge = edge_ref.at[BENT.index(d)] if cy != 0 else None
-        spread(d, plane, res.at[j], edge, yp_ref, ym_ref, zp_ref, zm_ref)
+        spread(d, lambda z: patched(rel, cols, j, z, 0, CY), res.at[j], edge, None)
         first, count = (1, CZ - 1) if cz > 0 else (0, CZ - 1) if cz < 0 else (0, CZ)
         planes = pl.ds(first, count)
         copy = pltpu.make_async_copy(res.at[j, planes], new_hbm.at[d, planes], sem.at[j])
         copy.start()
         copies.append(copy)
-    w_copy.wait()
+    place = place_ref[...].astype(jnp.bfloat16)
+    for k in range(3):
+        arrived = jnp.concatenate(
+            [in_ref[pl.ds(3 * r + k, OWNERS, stride=BACK_ROWS), :] for r in range(2)], axis=0
+        )
+        nodes[pl.ds(k, NB, stride=8), :] = jnp.dot(
+            place, arrived.astype(jnp.bfloat16), preferred_element_type=jnp.float32
+        )
+    for b in range(NB):
+        if b % (NB // parts) == 0:
+            w_copies[b // (NB // parts)].wait()
+        motion = lax.dot_general(
+            nodes[b * 8 : b * 8 + 8, :].astype(jnp.bfloat16),
+            w[b],
+            (((1,), (1,)), ((), ())),
+            preferred_element_type=jnp.float32,
+        )
+        out_ref[:, b, :] = motion[:3]
     for copy in copies:
         copy.wait()
 
 
-def stream_step(new, weights, moving, below, above, faces):
+def bulk_step(new, weights, moving, cols, place, arrived):
     return pl.pallas_call(
-        stream_body,
-        out_shape=(
-            shape((19, CZ, CY, CX)),
-            near((CZ, 8, CX)),
-            near((CZ, 8, CX)),
-            near((5, CY, CX)),
-            near((5, CY, CX)),
-            near((4, CZ, 8, CX)),
-            pltpu.VMEM((NEAR_BLOCKS, CX, SN), jnp.bfloat16),
-        ),
-        in_specs=[ANY] * 2 + [VMEM] * 7,
-        out_specs=(ANY,) + (VMEM,) * 6,
+        bulk_body,
+        out_shape=(shape((19, CZ, CY, CX)), near((4, CZ, 8, CX)), shape((3, NB, CX))),
+        in_specs=[ANY] * 2 + [VMEM] * 4,
+        out_specs=(ANY, VMEM, VMEM),
         input_output_aliases={0: 0},
         scratch_shapes=[
+            pltpu.VMEM((NB, CX, SN), jnp.bfloat16),
+            pltpu.VMEM((NB * 8, SN), jnp.float32),
             pltpu.VMEM((10, CZ, CY, CX), jnp.float32),
-            pltpu.VMEM((2, ROWS, 128), jnp.float32),
             pltpu.SemaphoreType.DMA((10,)),
-            pltpu.SemaphoreType.DMA,
+            pltpu.SemaphoreType.DMA((8,)),
         ],
-        cost_estimate=cost(10_000_000, 5_000_000),
+        cost_estimate=cost(30_000_000, 5_000_000),
         compiler_params=pltpu.CompilerParams(vmem_limit_bytes=16 * 1024 * 1024),
-        name="stream",
-    )(new, far(weights), held(moving), held(below), held(above), *[held(f) for f in faces])
+        name="bulk",
+    )(new, far(weights), held(moving), held(cols), held(place), held(arrived))
 
 
 def finish_body(
@@ -683,15 +679,13 @@
         incoming.reshape(OWNERS * OUT_ROWS, 128), compliance, neighbour_compliance, lines
     )
     arrived = exchange(back.reshape(OWNERS, 1, BACK_ROWS * 128))
-    new, yp, ym, zp, zm, bent, weights = stream_step(
-        new, rbf_weights, relaxed, xlo, xhi, (yp, ym, zp, zm)
-    )
+    yp, ym, zp, zm, cols = faces_step(relaxed, xlo, xhi, (yp, ym, zp, zm))
     ylo = from_behind(yp, "gy", 1)
     yhi = from_behind(ym, "gy", -1)
     zlo = from_behind(zp, "gz", 1)
     zhi = from_behind(zm, "gz", -1)
     arrived = arrived.reshape(OWNERS * BACK_ROWS, 128)
-    wall_motion = wall_step(place, arrived, weights, rbf_weights)
+    new, bent, wall_motion = bulk_step(new, rbf_weights, relaxed, cols, place, arrived)
     new = finish_step(new, still, bent, ylo, yhi, zlo, zhi, arrived)
     return (new, displacement.transpose(1, 0, 2), wall_motion.transpose(1, 0, 2))
 

time: 54.6 us -> 53.8 us (0.985)
  waiting for transfers between devices: 9.83 us -> 9.02 us
    ppermute x6, waiting for transfers between devices: 3.85 us -> 3.04 us  [from_behind(): return lax.ppermute(value, axis, pairs)]
    pallas_call x1, Pallas kernels: 4.23 us -> 4.81 us  [send_forces(): pl.pallas_call(forces_body, out_shape=(near((OWNERS * OUT_ROWS, 128)), ne...]
    pallas_call x2, Pallas kernels: 4.85 us -> 4.28 us  [the longest x1 4.04 us: bulk_step(): pl.pallas_call(bulk_body, out_shape=(shape((19, CZ, CY, CX)), near((4, CZ...]
  transfers between devices with their start and end apart: 8 -> 8, of which waited for: 3 -> 2; matrix products, arithmetic and copies ran while one was open for 0% -> 0% of each run, Pallas kernels for 16% -> 15%
where the time goes in v3:
time: 53.8 us; the launch traced here: 53.5 us
  starting transfers between devices  28.5 us (53%)
  Pallas kernels  15.2 us (28%)
  waiting for transfers between devices  9.02 us (17%)
  between operations  0.73 us (1%)
    all_to_all x2, starting transfers between devices, exchange(): lax.all_to_all(value, ('gy', 'gz'), split_axis=0, concat_axis=0, tiled=True)  15.8 us
    ppermute x6, starting transfers between devices, from_behind(): return lax.ppermute(value, axis, pairs)  12.7 us
    all_to_all x2, waiting for transfers between devices, exchange(): lax.all_to_all(value, ('gy', 'gz'), split_axis=0, concat_axis=0, tiled=True)  5.98 us
    pallas_call x1, Pallas kernels, send_forces(): pl.pallas_call(forces_body, out_shape=(near((OWNERS * OUT_ROWS, 128)), ne...  4.81 us
    pallas_call x1, Pallas kernels, bulk_step(): pl.pallas_call(bulk_body, out_shape=(shape((19, CZ, CY, CX)), near((4, CZ...  4.04 us
    pallas_call x1, Pallas kernels, collide_step(): pl.pallas_call(collide_body, out_shape=(shape((19, CZ, CY, CX)), near((10...  3.74 us
    ppermute x6, waiting for transfers between devices, from_behind(): return lax.ppermute(value, axis, pairs)  3.04 us
    pallas_call x1, Pallas kernels, owner_step(): pl.pallas_call(owner_body, out_shape=(shape((3, SB, SN)), near((OWNERS *...  1.43 us
  transfers between devices with their start and end apart: 8, of which 2 were waited for; matrix products, arithmetic and copies ran while one was open for 0% of the time, Pallas kernels for 15%

profile of v3, /device:TPU:1, one launch (start us, length us, event | category | flops | bytes accessed | tf_op | source)
XLA Modules:
  0.0 53.5 jit_solution(10234894219006148060)
XLA Ops:
  0.6 4.8 %forces.1 = (f32[640,128]{1,0:T(8,128)}, f32[19,64,128]{2,1,0:T(8,128)S(1)}, f32[64,128]{1,0:T(8,128)S(1)}) custom-call(s32[64]{0:T(128)} %row_hbm.1, s32[1,64]{1,0:T(1,128)} %bitcast.13, s32[1,64]{1,0:T(1,128)} %bitcast.14, f32[19,256,128]{2,1,0:T(8,128)} %bitcast.12, bf16[64,128,128]{2,1,0:T(8,128)(2,1)} %w_hbm.3), custom_call_target="tpu_custom_call" | custom-call | flops 50000000 | bytes 5000000 | tf_op jit(solution)/shard_map/forces/pallas_call | solution.py:202
  5.4 0.0 copy-start
  5.5 0.0 copy-start.1
  5.5 10.5 %all-to-all-start = ((f32[64,1,1280]{2,1,0:T(1,128)}), f32[64,1,1280]{2,1,0:T(1,128)S(1)}, u32[]{:S(2)}, u32[]{:S(2)}) async-start(f32[64,1,1280]{2,1,0:T(1,128)} %bitcast.3), calls=%async_computation | async-start | bytes 655360 | tf_op jit(solution)/shard_map/all_to_all | solution.py:663
  16.0 3.7 %collide.1 = (f32[19,8,32,128]{3,2,1,0:T(8,128)}, f32[10,8,32,128]{3,2,1,0:T(8,128)S(1)}, f32[8,256]{1,0:T(8,128)S(1)}, f32[8,256]{1,0:T(8,128)S(1)}, f32[8,8,12...) custom-call(f32[19,8,32,128]{3,2,1,0:T(8,128)} %pop_hbm.1, ...), custom_call_target="tpu_custom_call" | custom-call | flops 10000000 | bytes 5000000 | tf_op jit(solution)/shard_map/collide/pallas_call | solution.py:441
  19.7 6.0 %all-to-all-done = f32[64,1,1280]{2,1,0:T(1,128)S(1)} async-done(((f32[64,1,1280]{2,1,0:T(1,128)}), f32[64,1,1280]{2,1,0:T(1,128)S(1)}, u32[]{:S(2)}, u32[]{:S(2)}) %all-to-all-start) | async-done | bytes 327712 | tf_op jit(solution)/shard_map/all_to_all | solution.py:663
  25.7 0.0 copy-done
  25.7 0.0 copy-done.1
  25.7 1.4 %owner.1 = (f32[3,8,128]{2,1,0:T(8,128)}, f32[448,128]{1,0:T(8,128)}) custom-call(f32[640,128]{1,0:T(8,128)S(1)} %bitcast.11, f32[8,128,128]{2,1,0:T(8,128)S(1)} %copy-done, f32[128,128]{1,0:T(8,128)S(1)} %copy-done.1, f32[8,128]{1,0:T(8,128)S(1)} %get-tuple-element.38.yz_ref), custom_call_target="tpu_custom_call" | custom-call | flops 20000000 | bytes 1200000 | tf_op jit(solution)/shard_map/owner/pallas_call | solution.py:295
  27.1 5.4 %all-to-all-start.1 = ((f32[64,1,896]{2,1,0:T(1,128)}), f32[64,1,896]{2,1,0:T(1,128)S(1)}, u32[]{:S(2)}, u32[]{:S(2)}) async-start(f32[64,1,896]{2,1,0:T(1,128)} %bitcast.5), calls=%async_computation.1 | async-start | bytes 458752 | tf_op jit(solution)/shard_map/all_to_all | solution.py:663
  32.5 3.1 %collective-permute-start = (f32[8,256]{1,0:T(8,128)S(1)}, f32[8,256]{1,0:T(8,128)S(1)}, u32[]{:S(2)}, u32[]{:S(2)}) collective-permute-start(f32[8,256]{1,0:T(8,128)S(1)} %get-tuple-element.29), channel_id=1, source_target_pairs={{0,64},{64,128},{128,192},{192,0},{1,65},{65,129},{129,193},{193,1... | collective-permute-start | bytes 24584 | tf_op jit(solution)/shard_map/ppermute | solution.py:659
  35.5 2.2 %collective-permute-start.1 = (f32[8,256]{1,0:T(8,128)S(1)}, f32[8,256]{1,0:T(8,128)S(1)}, u32[]{:S(2)}, u32[]{:S(2)}) collective-permute-start(f32[8,256]{1,0:T(8,128)S(1)} %get-tuple-element.30), channel_id=1, source_target_pairs={{0,192},{64,0},{128,64},{192,128},{1,193},{65,1},{129,65},{193,129... | collective-permute-start | bytes 24584 | tf_op jit(solution)/shard_map/ppermute | solution.py:659
  37.8 3.0 %collective-permute-done.lo_ref = f32[8,256]{1,0:T(8,128)S(1)} collective-permute-done((f32[8,256]{1,0:T(8,128)S(1)}, f32[8,256]{1,0:T(8,128)S(1)}, u32[]{:S(2)}, u32[]{:S(2)}) %collective-permute-start) | collective-permute-done | bytes 8224 | tf_op jit(solution)/shard_map/ppermute | solution.py:659
  40.8 0.0 collective-permute-done.1.hi_ref
  40.8 0.2 faces.1
  41.1 1.5 %collective-permute-start.4 = (f32[5,32,128]{2,1,0:T(8,128)S(1)}, f32[5,32,128]{2,1,0:T(8,128)S(1)}, u32[]{:S(2)}, u32[]{:S(2)}) collective-permute-start(f32[5,32,128]{2,1,0:T(8,128)S(1)} %get-tuple-element.45), channel_id=1, source_target_pairs={{0,1},{1,2},{2,3},{3,4},{4,5},{5,6},{6,7},{7,8},{8,9},{9,10},{10,1... | collective-permute-start | bytes 245768 | tf_op jit(solution)/shard_map/ppermute | solution.py:659
  42.6 3.4 %collective-permute-start.5 = (f32[5,32,128]{2,1,0:T(8,128)S(1)}, f32[5,32,128]{2,1,0:T(8,128)S(1)}, u32[]{:S(2)}, u32[]{:S(2)}) collective-permute-start(f32[5,32,128]{2,1,0:T(8,128)S(1)} %get-tuple-element.46), channel_id=1, source_target_pairs={{0,15},{1,0},{2,1},{3,2},{4,3},{5,4},{6,5},{7,6},{8,7},{9,8},{10,9... | collective-permute-start | bytes 245768 | tf_op jit(solution)/shard_map/ppermute | solution.py:659
  45.9 2.5 %collective-permute-start.2 = (f32[8,8,128]{2,1,0:T(8,128)S(1)}, f32[8,8,128]{2,1,0:T(8,128)S(1)}, u32[]{:S(2)}, u32[]{:S(2)}) collective-permute-start(f32[8,8,128]{2,1,0:T(8,128)S(1)} %get-tuple-element.43), channel_id=1, source_target_pairs={{0,16},{16,32},{32,48},{48,0},{1,17},{17,33},{33,49},{49,1},{2,18}... | collective-permute-start | bytes 98312 | tf_op jit(solution)/shard_map/ppermute | solution.py:659
  48.5 0.0 collective-permute-start.3
  48.5 0.0 all-to-all-done.1
  48.5 4.0 %bulk.1 = (f32[19,8,32,128]{3,2,1,0:T(8,128)}, f32[4,8,8,128]{3,2,1,0:T(8,128)S(1)}, f32[3,64,128]{2,1,0:T(8,128)}) custom-call(f32[19,8,32,128]{3,2,1,0:T(8,128)} %get-tuple-element.27.new_in, bf16[64,128,128]{2,1,0:T(8,128)(2,1)} %w_hbm.3, f32[10,8,32,128]{3,2,1,0:T(8,128)S(1)} %get-tuple-element.28.rel, ...), custom_call_target="tpu_custom_call", output_to_operand_aliasing={{0}: (0, {})} | custom-call | flops 30000000 | bytes 5000000 | tf_op jit(solution)/shard_map/bulk/pallas_call | solution.py:581
  52.5 0.0 collective-permute-done.2.ylo
  52.5 0.0 collective-permute-done.3.yhi
  52.5 0.0 collective-permute-done.4.zlo
  52.5 0.0 collective-permute-done.5.zhi
  52.6 0.9 %finish.1 = f32[19,8,32,128]{3,2,1,0:T(8,128)} custom-call(f32[19,8,32,128]{3,2,1,0:T(8,128)} %get-tuple-element.40.new_in, f32[6,8,8,128]{3,2,1,0:T(8,128)S(1)} %get-tuple-element.41.still_ref, f32[4,8,8,128]{3,2,1,0:T(8,128)S(1)} %get-tuple-element.42.moving_ref, f32[8,8,128]{2,1,0:T(8,128)S(1)} %collective-permute-done.2.ylo, ...), custom_call_target="tpu_custom_call", output_to_operand_aliasing={{}: (0, {})} | custom-call | flops 100000 | bytes 1000000 | tf_op jit(solution)/shard_map/finish/pallas_call | solution.py:639
Async XLA Ops:
  5.4 20.2 %copy-start = (f32[8,128,128]{2,1,0:T(8,128)S(1)}, f32[8,128,128]{2,1,0:T(8,128)}, u32[]{:S(2)}) copy-start(f32[8,128,128]{2,1,0:T(8,128)} %comp_ref.1) | copy-start | bytes 1572868
  5.5 20.2 %copy-start.1 = (f32[128,128]{1,0:T(8,128)S(1)}, f32[128,128]{1,0:T(8,128)}, u32[]{:S(2)}) copy-start(f32[128,128]{1,0:T(8,128)} %near_ref.1) | copy-start | bytes 196612
  5.5 20.2 %all-to-all-start = ((f32[64,1,1280]{2,1,0:T(1,128)}), f32[64,1,1280]{2,1,0:T(1,128)S(1)}, u32[]{:S(2)}, u32[]{:S(2)}) async-start(f32[64,1,1280]{2,1,0:T(1,128)} %bitcast.3), calls=%async_computation | async-start | bytes 655360 | tf_op jit(solution)/shard_map/all_to_all | solution.py:663
  27.1 21.3 %all-to-all-start.1 = ((f32[64,1,896]{2,1,0:T(1,128)}), f32[64,1,896]{2,1,0:T(1,128)S(1)}, u32[]{:S(2)}, u32[]{:S(2)}) async-start(f32[64,1,896]{2,1,0:T(1,128)} %bitcast.5), calls=%async_computation.1 | async-start | bytes 458752 | tf_op jit(solution)/shard_map/all_to_all | solution.py:663
  32.5 8.3 %collective-permute-start = (f32[8,256]{1,0:T(8,128)S(1)}, f32[8,256]{1,0:T(8,128)S(1)}, u32[]{:S(2)}, u32[]{:S(2)}) collective-permute-start(f32[8,256]{1,0:T(8,128)S(1)} %get-tuple-element.29), channel_id=1, source_target_pairs={{0,64},{64,128},{128,192},{192,0},{1,65},{65,129},{129,193},{193,1... | collective-permute-start | bytes 24584 | tf_op jit(solution)/shard_map/ppermute | solution.py:659
  35.5 5.3 %collective-permute-start.1 = (f32[8,256]{1,0:T(8,128)S(1)}, f32[8,256]{1,0:T(8,128)S(1)}, u32[]{:S(2)}, u32[]{:S(2)}) collective-permute-start(f32[8,256]{1,0:T(8,128)S(1)} %get-tuple-element.30), channel_id=1, source_target_pairs={{0,192},{64,0},{128,64},{192,128},{1,193},{65,1},{129,65},{193,129... | collective-permute-start | bytes 24584 | tf_op jit(solution)/shard_map/ppermute | solution.py:659
  41.1 11.5 %collective-permute-start.4 = (f32[5,32,128]{2,1,0:T(8,128)S(1)}, f32[5,32,128]{2,1,0:T(8,128)S(1)}, u32[]{:S(2)}, u32[]{:S(2)}) collective-permute-start(f32[5,32,128]{2,1,0:T(8,128)S(1)} %get-tuple-element.45), channel_id=1, source_target_pairs={{0,1},{1,2},{2,3},{3,4},{4,5},{5,6},{6,7},{7,8},{8,9},{9,10},{10,1... | collective-permute-start | bytes 245768 | tf_op jit(solution)/shard_map/ppermute | solution.py:659
  42.6 10.0 %collective-permute-start.5 = (f32[5,32,128]{2,1,0:T(8,128)S(1)}, f32[5,32,128]{2,1,0:T(8,128)S(1)}, u32[]{:S(2)}, u32[]{:S(2)}) collective-permute-start(f32[5,32,128]{2,1,0:T(8,128)S(1)} %get-tuple-element.46), channel_id=1, source_target_pairs={{0,15},{1,0},{2,1},{3,2},{4,3},{5,4},{6,5},{7,6},{8,7},{9,8},{10,9... | collective-permute-start | bytes 245768 | tf_op jit(solution)/shard_map/ppermute | solution.py:659
  45.9 6.6 %collective-permute-start.2 = (f32[8,8,128]{2,1,0:T(8,128)S(1)}, f32[8,8,128]{2,1,0:T(8,128)S(1)}, u32[]{:S(2)}, u32[]{:S(2)}) collective-permute-start(f32[8,8,128]{2,1,0:T(8,128)S(1)} %get-tuple-element.43), channel_id=1, source_target_pairs={{0,16},{16,32},{32,48},{48,0},{1,17},{17,33},{33,49},{49,1},{2,18}... | collective-permute-start | bytes 98312 | tf_op jit(solution)/shard_map/ppermute | solution.py:659
  48.5 4.1 %collective-permute-start.3 = (f32[8,8,128]{2,1,0:T(8,128)S(1)}, f32[8,8,128]{2,1,0:T(8,128)S(1)}, u32[]{:S(2)}, u32[]{:S(2)}) collective-permute-start(f32[8,8,128]{2,1,0:T(8,128)S(1)} %get-tuple-element.44), channel_id=1, source_target_pairs={{0,48},{16,0},{32,16},{48,32},{1,49},{17,1},{33,17},{49,33},{2,50}... | collective-permute-start | bytes 98312 | tf_op jit(solution)/shard_map/ppermute | solution.py:659
